TPU v7x, 256 devices: a whole 4x4x8 slice. The times are simulated.
256 devices in a mesh: grp: 4 (over x), tile: 64 (over z, y, core).
Axes of the slice: x: 4, y: 4, z: 8, core: 2. Of those that a mesh axis runs over, the one named last changes fastest.
Arguments:
- bricks: float32 [512, 128, 512], P(('grp', 'tile')), may hold values from 0 to 1
- colour_table: float32 [3, 256], replicated, may hold values from 0.5 to 8
- opacity_table: float32 [256], replicated, may hold values from 2e-05 to 0.005
- depth_order: int32 [4, 64], replicated, may hold values from 0 to 63, each once within a row
Outputs:
- image: float32 [4, 65536], P(None, ('grp', 'tile'))
Inputs may be any that keep to these rules, and one draw needn't show every extreme that they name: Each row of depth_order holds every number 0 .. 63 once.
All inputs are finite; a program needn't handle non-finite values.
Results may differ from a plain program's by a relative error of at most 0.0003.
Values sent between devices are 32-bit elements; how exact they have to be, the bound alone decides.
A program may use at most 64 MiB of HBM per device.

v0:
```python
import jax
import jax.numpy as jnp
from jax import lax
from jax.sharding import PartitionSpec as P


def shade_cells(values, palette):
    knot_count = palette.shape[1]
    position = values * (knot_count - 1)
    knot_pos = lax.broadcasted_iota(jnp.float32, (knot_count, 1), 0)
    weights = jnp.maximum(0.0, 1.0 - jnp.abs(position[None, :] - knot_pos))
    return jnp.dot(
        palette, weights, precision=lax.Precision.HIGHEST, preferred_element_type=jnp.float32
    )


def render(bricks, palette):
    depth_count = bricks.shape[0]
    pixels = bricks.shape[1] * bricks.shape[2]
    slices = bricks.reshape(depth_count, pixels)
    block_len = pixels // 8

    def one_slice(depth_at, carry):
        colour, transmit = carry
        values = lax.dynamic_index_in_dim(slices, depth_at, 0, keepdims=False)
        shaded = [
            shade_cells(lax.slice_in_dim(values, j * block_len, (j + 1) * block_len), palette)
            for j in range(8)
        ]
        sample = jnp.concatenate(shaded, axis=1)
        weight = transmit * sample[3]
        colour = colour + weight[None, :] * sample[:3]
        transmit = transmit * (1.0 - sample[3])
        return (colour, transmit)

    start = (jnp.zeros((3, pixels), jnp.float32), jnp.ones((pixels,), jnp.float32))
    colour, transmit = lax.fori_loop(0, depth_count, one_slice, start)
    return jnp.concatenate([colour, (1.0 - transmit)[None, :]], axis=0)


def composite(layers):
    while layers.shape[0] > 1:
        near_half = layers[0::2]
        far_half = layers[1::2]
        layers = near_half + (1.0 - near_half[:, 3:4]) * far_half
    return layers[0]


def body(bricks, colour_table, opacity_table, depth_order):
    palette = jnp.concatenate([colour_table, opacity_table[None, :]], axis=0)
    partial_value = render(bricks, palette)
    groups = lax.axis_size("grp")
    members = lax.axis_size("tile")
    pixels = partial_value.shape[1]
    sub_len = pixels // (groups * members)
    sectioned = partial_value.reshape(1, 4, groups, members, sub_len)
    layers = lax.all_to_all(sectioned, "tile", split_axis=3, concat_axis=0, tiled=True)
    layers = layers.reshape(members, 4, groups, sub_len)
    group_index = lax.axis_index("grp")
    rank_row = lax.dynamic_index_in_dim(depth_order, group_index, 0, keepdims=False)
    by_rank = jnp.argsort(rank_row)
    ordered = jnp.take(layers, by_rank, axis=0)
    own_group = composite(ordered)
    arrived = lax.all_to_all(own_group[None], "grp", split_axis=2, concat_axis=0, tiled=True)
    result = composite(arrived).reshape(4, sub_len)
    return result


def solution(mesh):
    in_specs = (P(("grp", "tile"), None, None), P(), P(), P())
    out_specs = P(None, ("grp", "tile"))
    return jax.shard_map(body, mesh=mesh, in_specs=in_specs, out_specs=out_specs, check_vma=False)
```

profile of v0, /device:TPU:1, one launch (start us, length us, event | category | flops | bytes accessed | tf_op | source)
XLA Modules:
  0.0 152.1 jit_solution(6230588998813952491)
XLA Ops:
  0.0 0.0 copy-start
  0.0 0.0 copy-start.2
  0.0 0.0 copy-start.1
  0.0 1.5 copy.10
  1.5 0.0 copy-done.2
  1.5 0.0 copy-done.1
  1.5 96.2 %while.16 = (s32[]{:T(128)}, f32[3,65536]{1,0:T(4,128)S(1)}, f32[65536]{0:T(1024)S(1)}, f32[2,65536]{1,0:T(2,128)S(1)}, f32[4,256]{1,0:T(4,128)S(1)}, /*index=5*...) while((s32[]{:T(128)}, f32[3,65536]{1,0:T(4,128)S(1)}, ...), condition=%wide.region_2.3_spmd.clone, body=%wide.region_1.2_spmd.clone.sunk | while | flops 873332736 | bytes 6062348 | solution.py:37
  1.8 0.6 dynamic-slice_multiply_fusion.9
  2.3 5.4 %fusion.147 = f32[4,65536]{1,0:T(4,128)S(1)} fusion(f32[4,256]{1,0:T(4,128)S(1)} %get-tuple-element.225, f32[8192]{0:T(1024)S(1)} %bitcast.147), kind=kOutput, calls=%fused_computation.16.clone.1 | convolution fusion | flops 109051904 | bytes 167936 | tf_op jit(solution)/shard_map/while/body/eval_jaxpr/dot_general | solution.py:12
  7.8 5.4 %fusion.148 = f32[4,65536]{1,0:T(4,128)S(1)} fusion(f32[4,65536]{1,0:T(4,128)S(1)} %fusion.147, f32[4,256]{1,0:T(4,128)S(1)} %get-tuple-element.225, f32[8192]{0:T(1024)S(1)} %bitcast.146), kind=kOutput, calls=%fused_computation.14.clone.1 | convolution fusion | flops 109051904 | bytes 167936 | tf_op jit(solution)/shard_map/while/body/eval_jaxpr/dot_general | solution.py:12
  13.2 6.0 %fusion.149 = f32[4,65536]{1,0:T(4,128)S(1)} fusion(f32[4,65536]{1,0:T(4,128)S(1)} %fusion.148, f32[4,256]{1,0:T(4,128)S(1)} %get-tuple-element.225, f32[8192]{0:T(1024)S(1)} %bitcast.145), kind=kOutput, calls=%fused_computation.12.clone.1 | convolution fusion | flops 109051904 | bytes 167936 | tf_op jit(solution)/shard_map/while/body/eval_jaxpr/dot_general | solution.py:12
  19.2 5.4 %fusion.150 = f32[4,65536]{1,0:T(4,128)S(1)} fusion(f32[4,65536]{1,0:T(4,128)S(1)} %fusion.149, f32[4,256]{1,0:T(4,128)S(1)} %get-tuple-element.225, f32[8192]{0:T(1024)S(1)} %bitcast.144), kind=kOutput, calls=%fused_computation.10.clone.1 | convolution fusion | flops 109051904 | bytes 167936 | tf_op jit(solution)/shard_map/while/body/eval_jaxpr/dot_general | solution.py:12
  24.6 5.6 %fusion.151 = f32[4,65536]{1,0:T(4,128)S(1)} fusion(f32[4,65536]{1,0:T(4,128)S(1)} %fusion.150, f32[4,256]{1,0:T(4,128)S(1)} %get-tuple-element.225, f32[8192]{0:T(1024)S(1)} %bitcast.143), kind=kOutput, calls=%fused_computation.8.clone.1 | convolution fusion | flops 109051904 | bytes 167936 | tf_op jit(solution)/shard_map/while/body/eval_jaxpr/dot_general | solution.py:12
  30.2 5.4 %fusion.152 = f32[4,65536]{1,0:T(4,128)S(1)} fusion(f32[4,65536]{1,0:T(4,128)S(1)} %fusion.151, f32[4,256]{1,0:T(4,128)S(1)} %get-tuple-element.225, f32[8192]{0:T(1024)S(1)} %bitcast.142), kind=kOutput, calls=%fused_computation.6.clone.1 | convolution fusion | flops 109051904 | bytes 167936 | tf_op jit(solution)/shard_map/while/body/eval_jaxpr/dot_general | solution.py:12
  35.7 5.7 %fusion.153 = f32[4,65536]{1,0:T(4,128)S(1)} fusion(f32[4,65536]{1,0:T(4,128)S(1)} %fusion.152, f32[4,256]{1,0:T(4,128)S(1)} %get-tuple-element.225, f32[8192]{0:T(1024)S(1)} %bitcast.141), kind=kOutput, calls=%fused_computation.4.clone.1 | convolution fusion | flops 109051904 | bytes 167936 | tf_op jit(solution)/shard_map/while/body/eval_jaxpr/dot_general | solution.py:12
  41.3 5.4 %fusion.154 = f32[4,65536]{1,0:T(4,128)S(1)} fusion(f32[4,65536]{1,0:T(4,128)S(1)} %fusion.153, f32[4,256]{1,0:T(4,128)S(1)} %get-tuple-element.225, f32[8192]{0:T(1024)S(1)} %bitcast.140), kind=kOutput, calls=%fused_computation.2.clone.1 | convolution fusion | flops 109051904 | bytes 167936 | tf_op jit(solution)/shard_map/while/body/eval_jaxpr/dot_general | solution.py:12
  46.8 0.3 slice.255
  47.1 0.2 subtract_multiply_fusion.2
  47.2 0.6 fusion.155
  48.3 0.6 dynamic-slice_multiply_fusion.9
  48.8 5.4 %fusion.147 = f32[4,65536]{1,0:T(4,128)S(1)} fusion(f32[4,256]{1,0:T(4,128)S(1)} %get-tuple-element.225, f32[8192]{0:T(1024)S(1)} %bitcast.147), kind=kOutput, calls=%fused_computation.16.clone.1 | convolution fusion | flops 109051904 | bytes 167936 | tf_op jit(solution)/shard_map/while/body/eval_jaxpr/dot_general | solution.py:12
  54.2 5.4 %fusion.148 = f32[4,65536]{1,0:T(4,128)S(1)} fusion(f32[4,65536]{1,0:T(4,128)S(1)} %fusion.147, f32[4,256]{1,0:T(4,128)S(1)} %get-tuple-element.225, f32[8192]{0:T(1024)S(1)} %bitcast.146), kind=kOutput, calls=%fused_computation.14.clone.1 | convolution fusion | flops 109051904 | bytes 167936 | tf_op jit(solution)/shard_map/while/body/eval_jaxpr/dot_general | solution.py:12
  59.7 5.6 %fusion.149 = f32[4,65536]{1,0:T(4,128)S(1)} fusion(f32[4,65536]{1,0:T(4,128)S(1)} %fusion.148, f32[4,256]{1,0:T(4,128)S(1)} %get-tuple-element.225, f32[8192]{0:T(1024)S(1)} %bitcast.145), kind=kOutput, calls=%fused_computation.12.clone.1 | convolution fusion | flops 109051904 | bytes 167936 | tf_op jit(solution)/shard_map/while/body/eval_jaxpr/dot_general | solution.py:12
  65.3 5.4 %fusion.150 = f32[4,65536]{1,0:T(4,128)S(1)} fusion(f32[4,65536]{1,0:T(4,128)S(1)} %fusion.149, f32[4,256]{1,0:T(4,128)S(1)} %get-tuple-element.225, f32[8192]{0:T(1024)S(1)} %bitcast.144), kind=kOutput, calls=%fused_computation.10.clone.1 | convolution fusion | flops 109051904 | bytes 167936 | tf_op jit(solution)/shard_map/while/body/eval_jaxpr/dot_general | solution.py:12
  70.8 5.7 %fusion.151 = f32[4,65536]{1,0:T(4,128)S(1)} fusion(f32[4,65536]{1,0:T(4,128)S(1)} %fusion.150, f32[4,256]{1,0:T(4,128)S(1)} %get-tuple-element.225, f32[8192]{0:T(1024)S(1)} %bitcast.143), kind=kOutput, calls=%fused_computation.8.clone.1 | convolution fusion | flops 109051904 | bytes 167936 | tf_op jit(solution)/shard_map/while/body/eval_jaxpr/dot_general | solution.py:12
  76.4 5.4 %fusion.152 = f32[4,65536]{1,0:T(4,128)S(1)} fusion(f32[4,65536]{1,0:T(4,128)S(1)} %fusion.151, f32[4,256]{1,0:T(4,128)S(1)} %get-tuple-element.225, f32[8192]{0:T(1024)S(1)} %bitcast.142), kind=kOutput, calls=%fused_computation.6.clone.1 | convolution fusion | flops 109051904 | bytes 167936 | tf_op jit(solution)/shard_map/while/body/eval_jaxpr/dot_general | solution.py:12
  81.9 5.8 %fusion.153 = f32[4,65536]{1,0:T(4,128)S(1)} fusion(f32[4,65536]{1,0:T(4,128)S(1)} %fusion.152, f32[4,256]{1,0:T(4,128)S(1)} %get-tuple-element.225, f32[8192]{0:T(1024)S(1)} %bitcast.141), kind=kOutput, calls=%fused_computation.4.clone.1 | convolution fusion | flops 109051904 | bytes 167936 | tf_op jit(solution)/shard_map/while/body/eval_jaxpr/dot_general | solution.py:12
  87.7 5.4 %fusion.154 = f32[4,65536]{1,0:T(4,128)S(1)} fusion(f32[4,65536]{1,0:T(4,128)S(1)} %fusion.153, f32[4,256]{1,0:T(4,128)S(1)} %get-tuple-element.225, f32[8192]{0:T(1024)S(1)} %bitcast.140), kind=kOutput, calls=%fused_computation.2.clone.1 | convolution fusion | flops 109051904 | bytes 167936 | tf_op jit(solution)/shard_map/while/body/eval_jaxpr/dot_general | solution.py:12
  93.1 0.3 slice.255
  93.4 0.2 subtract_multiply_fusion.2
  93.6 0.6 fusion.155
  97.8 0.1 concatenate.20
  97.8 0.2 copy.11
  98.0 0.1 pad_maximum_fusion
  98.1 1.7 %copy.7 = f32[1,4,4,64,256]{4,2,1,0,3:T(4,128)} copy(f32[1,4,4,64,256]{4,3,2,1,0:T(8,128)S(1)} %pad_maximum_fusion) | data formatting | bytes 2097152 | tf_op jit(solution)/shard_map/concatenate | solution.py:38
  99.7 13.1 %all-to-all-start = ((f32[1,4,4,64,256]{4,2,1,0,3:T(4,128)}), f32[1,4,4,64,256]{4,2,1,0,3:T(4,128)S(1)}, u32[]{:S(2)}, u32[]{:S(2)}) async-start(f32[1,4,4,64,256]{4,2,1,0,3:T(4,128)} %copy.7), calls=%async_computation | async-start | bytes 2097152 | tf_op jit(solution)/shard_map/all_to_all | solution.py:57
  112.9 0.0 copy-done
  112.9 2.0 %sort.17 = (s32[64]{0:T(128)}, s32[64]{0:T(128)S(1)}) sort(s32[64]{0:T(128)S(1)} %dynamic-slice_bitcast_fusion, s32[64]{0:T(128)S(1)} %iota.12), dimensions={0}, to_apply=%region_0.1 | sort | flops 384 | bytes 1024 | tf_op jit(solution)/shard_map/jit(argsort)/sort | solution.py:61
  115.0 26.1 %all-to-all-done = f32[1,4,4,64,256]{4,2,1,0,3:T(4,128)S(1)} async-done(((f32[1,4,4,64,256]{4,2,1,0,3:T(4,128)}), f32[1,4,4,64,256]{4,2,1,0,3:T(4,128)S(1)}, u32[]{:S(2)}, u32[]{:S(2)}) %all-to-all-start) | async-done | bytes 1048608 | tf_op jit(solution)/shard_map/all_to_all | solution.py:57
  141.1 1.2 gather_fusion
  142.2 0.3 broadcast_select_fusion
  142.6 0.2 multiply_add_fusion
  142.9 0.1 multiply_add_fusion.1
  143.2 8.0 %all_to_all.33 = f32[1,4,4,256]{3,1,0,2:T(4,128)S(1)} all-to-all(f32[1,4,4,256]{3,1,0,2:T(4,128)S(1)} %copy.8), channel_id=1, replica_groups=mesh['grp'=4,'tile'=64] {'grp'}, dimensions={2} | all-to-all | bytes 32768 | tf_op jit(solution)/shard_map/all_to_all | solution.py:64
  151.3 0.6 fusion.96
  (30 shorter events, 0.3 us)
Async XLA Ops:
  0.0 112.9 %copy-start = (s32[4,64]{1,0:T(4,128)S(1)}, s32[4,64]{1,0:T(4,128)}, u32[]{:S(2)}) copy-start(s32[4,64]{1,0:T(4,128)} %param.9) | copy-start | bytes 3076
  0.0 1.5 copy-start.2
  0.0 1.5 copy-start.1
  99.7 41.3 %all-to-all-start = ((f32[1,4,4,64,256]{4,2,1,0,3:T(4,128)}), f32[1,4,4,64,256]{4,2,1,0,3:T(4,128)S(1)}, u32[]{:S(2)}, u32[]{:S(2)}) async-start(f32[1,4,4,64,256]{4,2,1,0,3:T(4,128)} %copy.7), calls=%async_computation | async-start | bytes 2097152 | tf_op jit(solution)/shard_map/all_to_all | solution.py:57
where the time goes:
time: 155 us; the launch traced here: 152 us
  matrix products  88.8 us (57%)
  waiting for transfers between devices  26.1 us (17%)
  starting transfers between devices  13.1 us (8%)
  blocking collectives  8.03 us (5%)
  other arithmetic  6.19 us (4%)
  local copies, waits for them, and re-layouts  5.18 us (3%)
  loops' own time  4.23 us (3%)
    dot_general x16, matrix products, shade_cells(): jnp.dot(palette, weights, precision=lax.Precision.HIGHEST, preferred_elem...  88.8 us
    all_to_all x1, waiting for transfers between devices, body(): lax.all_to_all(sectioned, 'tile', split_axis=3, concat_axis=0, tiled=True)  26.1 us
    all_to_all x1, starting transfers between devices, body(): lax.all_to_all(sectioned, 'tile', split_axis=3, concat_axis=0, tiled=True)  13.1 us
    all_to_all x1, blocking collectives, body(): lax.all_to_all(own_group[None], 'grp', split_axis=2, concat_axis=0, tiled...  8.03 us
    another operation x1, loops' own time, render(): colour, transmit = lax.fori_loop(0, depth_count, one_slice, start)  4.23 us
  transfers between devices with their start and end apart: 1, of which 1 were waited for; matrix products, arithmetic and copies ran while one was open for 1% of the time, Pallas kernels for 0%

commit v1 on v0

v1 whole, which is shorter than its diff:
```python
import jax
import jax.numpy as jnp
from jax import lax
from jax.experimental import pallas as pl
from jax.experimental.pallas import tpu as pltpu
from jax.sharding import PartitionSpec as P

LANES = 128
ROWS_PER_STEP = 8


def lookup_tables(palette):
    channels, knots = palette.shape
    extended = jnp.concatenate([palette, palette[:, -1:]], axis=1)
    halves = knots // LANES
    lower = extended[:, 0:knots].reshape(channels, halves, LANES)
    upper = extended[:, 1 : knots + 1].reshape(channels, halves, LANES)
    tables = jnp.stack([lower, upper], axis=1)
    tables = jnp.broadcast_to(tables[..., None, :], (channels, 2, halves, ROWS_PER_STEP, LANES))
    return tables.reshape(channels * 2 * halves, ROWS_PER_STEP, LANES)


def shade_kernel(knots, values_ref, tables_ref, out_ref):
    channels = out_ref.shape[0]
    bricks = values_ref.shape[1]
    width = values_ref.shape[2]
    halves = knots // LANES
    tables = [tables_ref[k] for k in range(tables_ref.shape[0])]

    def table(c, s, h):
        return tables[(c * 2 + s) * halves + h]

    def sample(v):
        u = v * float(knots - 1)
        lower = jnp.clip(jnp.floor(u), 0.0, float(knots - 2))
        frac = u - lower
        index = lower.astype(jnp.int32)
        lane = index % LANES
        half = index // LANES
        rows = []
        for c in range(channels):
            picked = []
            for s in range(2):
                got = jnp.take_along_axis(table(c, s, 0), lane, axis=1, mode="promise_in_bounds")
                for h in range(1, halves):
                    other = jnp.take_along_axis(table(c, s, h), lane, axis=1, mode="promise_in_bounds")
                    got = jnp.where(half == h, other, got)
                picked.append(got)
            rows.append(picked[0] * (1.0 - frac) + picked[1] * frac)
        return rows

    def step(i, carry):
        r0 = pl.multiple_of(i * ROWS_PER_STEP, ROWS_PER_STEP)
        for j in range(width // LANES):
            rs = pl.ds(r0, ROWS_PER_STEP)
            ls = pl.ds(j * LANES, LANES)
            colour = None
            transmit = None
            for d in range(values_ref.shape[0]):
                smp = sample(values_ref[d, rs, ls])
                alpha = smp[channels - 1]
                if d == 0:
                    colour = [alpha * smp[c] for c in range(channels - 1)]
                    transmit = 1.0 - alpha
                else:
                    weight = transmit * alpha
                    colour = [colour[c] + weight * smp[c] for c in range(channels - 1)]
                    transmit = transmit * (1.0 - alpha)
            for c in range(channels - 1):
                out_ref[c, rs, ls] = colour[c]
            out_ref[channels - 1, rs, ls] = 1.0 - transmit
        return carry

    lax.fori_loop(0, bricks // ROWS_PER_STEP, step, 0)


def shade_bricks(values, palette):
    depth, bricks, width = values.shape
    channels, knots = palette.shape
    tables = lookup_tables(palette)

    def kernel(values_ref, tables_ref, out_ref):
        shade_kernel(knots, values_ref, tables_ref, out_ref)

    return pl.pallas_call(
        kernel,
        out_shape=jax.ShapeDtypeStruct((channels, bricks, width), jnp.float32),
        in_specs=[
            pl.BlockSpec(memory_space=pltpu.VMEM),
            pl.BlockSpec(memory_space=pltpu.VMEM),
        ],
        out_specs=pl.BlockSpec(memory_space=pltpu.VMEM),
    )(values, tables)


def composite(layers):
    while layers.shape[1] > 1:
        near_half = layers[:, 0::2]
        far_half = layers[:, 1::2]
        layers = near_half + (1.0 - near_half[3:4]) * far_half
    return layers[:, 0]


def body(bricks, colour_table, opacity_table, depth_order):
    palette = jnp.concatenate([colour_table, opacity_table[None, :]], axis=0)
    groups = lax.axis_size("grp")
    members = lax.axis_size("tile")
    devices = groups * members
    depth = bricks.shape[0]
    pixels = bricks.shape[1] * bricks.shape[2]
    block = pixels // devices
    local = bricks.reshape(depth, devices, block)
    gathered = lax.all_to_all(local, ("grp", "tile"), 1, 1, tiled=True)
    partials = shade_bricks(gathered, palette)
    by_rank = jnp.argsort(depth_order, axis=1).astype(jnp.int32)
    sequence = (jnp.arange(groups, dtype=jnp.int32)[:, None] * members + by_rank).reshape(-1)
    ordered = jnp.take(partials, sequence, axis=1)
    return composite(ordered)


def solution(mesh):
    in_specs = (P(("grp", "tile"), None, None), P(), P(), P())
    out_specs = P(None, ("grp", "tile"))
    return jax.shard_map(body, mesh=mesh, in_specs=in_specs, out_specs=out_specs, check_vma=False)
```

time: 155 us -> 52.8 us (0.34); the launches traced: 152 us -> 52.5 us
  matrix products: 88.8 us -> 0 us
  waiting for transfers between devices: 26.1 us -> 17.8 us
  blocking collectives: 8.03 us -> 0 us
  Pallas kernels: 0 us -> 7.26 us
  loops' own time: 4.23 us -> 0 us
  local copies, waits for them, and re-layouts: 5.18 us -> 8.67 us
  other arithmetic: 6.19 us -> 2.82 us
  starting transfers between devices: 13.1 us -> 15.6 us
    dot_general x16 -> x0, matrix products: 88.8 us -> none  [shade_cells(): jnp.dot(palette, weights, precision=lax.Precision.HIGHEST, preferred_elem...]
    all_to_all x1, waiting for transfers between devices: 26.1 us -> 17.8 us  [body(): gathered = lax.all_to_all(local, ('grp', 'tile'), 1, 1, tiled=True)]
    all_to_all x1 -> x0, blocking collectives: 8.03 us -> none  [body(): lax.all_to_all(own_group[None], 'grp', split_axis=2, concat_axis=0, tiled...]
    pallas_call x0 -> x1, Pallas kernels: none -> 7.26 us  [shade_bricks(): pl.pallas_call(kernel, out_shape=jax.ShapeDtypeStruct((channels, bricks,...]
    another operation x1 -> x0, loops' own time: 4.23 us -> none  [render(): colour, transmit = lax.fori_loop(0, depth_count, one_slice, start)]
    all_to_all x1, starting transfers between devices: 13.1 us -> 15.6 us  [body(): gathered = lax.all_to_all(local, ('grp', 'tile'), 1, 1, tiled=True)]
    reshape x0 -> x4, local copies, waits for them, and re-layouts: none -> 2.49 us  [the longest x2 2.33 us: body(): local = bricks.reshape(depth, devices, block)]
    pallas_call x0 -> x1, local copies, waits for them, and re-layouts: none -> 1.9 us  [shade_bricks(): pl.pallas_call(kernel, out_shape=jax.ShapeDtypeStruct((channels, bricks,...]
  transfers between devices with their start and end apart: 1 -> 1, of which waited for: 1 -> 1; matrix products, arithmetic and copies ran while one was open for 1% -> 3% of each run, Pallas kernels for 0% -> 0%
where the time goes in v1:
time: 52.8 us; the launch traced here: 52.5 us
  waiting for transfers between devices  17.8 us (34%)
  starting transfers between devices  15.6 us (30%)
  local copies, waits for them, and re-layouts  8.67 us (16%)
  Pallas kernels  7.26 us (14%)
  other arithmetic  2.82 us (5%)
    all_to_all x1, waiting for transfers between devices, body(): gathered = lax.all_to_all(local, ('grp', 'tile'), 1, 1, tiled=True)  17.8 us
    all_to_all x1, starting transfers between devices, body(): gathered = lax.all_to_all(local, ('grp', 'tile'), 1, 1, tiled=True)  15.6 us
    pallas_call x1, Pallas kernels, shade_bricks(): pl.pallas_call(kernel, out_shape=jax.ShapeDtypeStruct((channels, bricks,...  7.26 us
    reshape x2, local copies, waits for them, and re-layouts, body(): local = bricks.reshape(depth, devices, block)  2.33 us
    pallas_call x1, local copies, waits for them, and re-layouts, shade_bricks(): pl.pallas_call(kernel, out_shape=jax.ShapeDtypeStruct((channels, bricks,...  1.9 us
    unnamed x14, local copies, waits for them, and re-layouts  1.34 us
    gather x1, local copies, waits for them, and re-layouts, body(): ordered = jnp.take(partials, sequence, axis=1)  1.26 us
  transfers between devices with their start and end apart: 1, of which 1 were waited for; matrix products, arithmetic and copies ran while one was open for 3% of the time, Pallas kernels for 0%

profile of v1, /device:TPU:1, one launch (start us, length us, event | category | flops | bytes accessed | tf_op | source)
XLA Modules:
  0.0 52.5 jit_solution(14724413840666947048)
XLA Ops:
  0.0 1.1 %reshape.57 = f32[2,256,256]{2,1,0:T(8,128)S(1)} reshape(f32[2,128,512]{2,1,0:T(8,128)} %param.4) | data formatting | bytes 1048576 | tf_op jit(solution)/shard_map/reshape | solution.py:112
  1.1 1.2 %copy.22 = f32[2,256,256]{2,0,1:T(2,128)} copy(f32[2,256,256]{2,1,0:T(8,128)S(1)} %reshape.57) | data formatting | bytes 1048576 | tf_op jit(solution)/shard_map/reshape | solution.py:112
  2.3 0.0 copy-start.2
  2.3 15.6 %all-to-all-start = ((f32[2,256,256]{2,0,1:T(2,128)}), f32[2,256,256]{2,0,1:T(2,128)S(1)}, u32[]{:S(2)}, u32[]{:S(2)}) async-start(f32[2,256,256]{2,0,1:T(2,128)} %copy.22), calls=%async_computation | async-start | bytes 1048576 | tf_op jit(solution)/shard_map/all_to_all | solution.py:113
  18.0 0.0 copy-done.2
  18.0 0.1 copy.20
  18.1 1.0 %sort.17 = (s32[4,64]{0,1:T(8,128)}, s32[4,64]{0,1:T(8,128)S(1)}) sort(s32[4,64]{0,1:T(8,128)S(1)} %copy.20, s32[4,64]{0,1:T(8,128)S(1)} %iota.13), dimensions={1}, to_apply=%region_0.0 | sort | flops 2048 | bytes 4096 | tf_op jit(solution)/shard_map/jit(argsort)/sort | solution.py:115
  19.1 0.1 copy.21
  19.2 0.0 copy-start
  19.2 0.1 reshape.58
  19.3 0.1 reshape.56
  19.4 0.5 %copy-done = f32[3,256]{1,0:T(4,128)S(1)} copy-done((f32[3,256]{1,0:T(4,128)S(1)}, f32[3,256]{1,0:T(4,128)}, u32[]{:S(2)}) %copy-start) | copy-done | bytes 3096
  19.9 0.0 copy-start.1
  19.9 0.7 %copy-done.1 = f32[256]{0:T(256)S(1)} copy-done((f32[256]{0:T(256)S(1)}, f32[256]{0:T(256)}, u32[]{:S(2)}) %copy-start.1) | copy-done | bytes 1048
  20.6 0.1 fusion.2
  20.7 17.8 %all-to-all-done = f32[2,256,256]{2,0,1:T(2,128)S(1)} async-done(((f32[2,256,256]{2,0,1:T(2,128)}), f32[2,256,256]{2,0,1:T(2,128)S(1)}, u32[]{:S(2)}, u32[]{:S(2)}) %all-to-all-start) | async-done | bytes 524320 | tf_op jit(solution)/shard_map/all_to_all | solution.py:113
  38.5 0.9 %copy.24.values_ref = f32[2,256,256]{2,1,0:T(8,128)} copy(f32[2,256,256]{2,0,1:T(2,128)S(1)} %all-to-all-done) | data formatting | bytes 1048576 | tf_op jit(solution)/shard_map/all_to_all | solution.py:113
  39.4 0.6 %broadcast_in_dim.25.tables_ref = f32[16,8,128]{2,1,0:T(8,128)} broadcast(f32[16,128]{1,0:T(8,128)S(1)} %bitcast.34), dimensions={0,2} | broadcast | bytes 73728 | tf_op jit(solution)/shard_map/broadcast_in_dim | solution.py:19
  40.0 7.3 %shard_map.46 = f32[4,256,256]{2,1,0:T(8,128)} custom-call(f32[2,256,256]{2,1,0:T(8,128)} %copy.24.values_ref, f32[16,8,128]{2,1,0:T(8,128)} %broadcast_in_dim.25.tables_ref), custom_call_target="tpu_custom_call" | custom-call | tf_op jit(solution)/shard_map/pallas_call | solution.py:85
  47.3 1.9 %copy.26 = f32[4,256,256]{2,0,1:T(4,128)S(1)} copy(f32[4,256,256]{2,1,0:T(8,128)} %shard_map.46) | data formatting | bytes 2097152 | tf_op jit(solution)/shard_map/pallas_call | solution.py:85
  49.2 1.3 %gather_fusion = f32[256,4,256]{2,1,0:T(4,128)S(1)} fusion(f32[4,256,256]{2,0,1:T(4,128)S(1)} %copy.26, s32[1024]{0:T(1024)S(1)} %pad_clamp_fusion), kind=kCustom, calls=%fused_computation | custom fusion | bytes 2098176 | tf_op jit(solution)/shard_map/jit(_take)/gather | solution.py:117
  50.4 0.3 select_bitcast_fusion
  50.8 0.2 slice_subtract_fusion
  51.0 0.2 multiply_add_fusion
  51.2 0.1 slice_subtract_fusion.1
  51.4 0.1 multiply_add_fusion.1
  51.9 0.6 %fusion.1 = f32[4,256]{1,0:T(4,128)} fusion(f32[4,2,256]{2,0,1:T(4,128)S(1)} %multiply_add_fusion.6, f32[256]{0:T(256)S(1)} %bitcast.41), kind=kLoop, calls=%fused_computation.24 | loop fusion | flops 2048 | bytes 13312 | tf_op jit(solution)/shard_map/squeeze | solution.py:101
  (35 shorter events, 0.4 us)
Async XLA Ops:
  2.3 15.7 %copy-start.2 = (s32[4,64]{1,0:T(4,128)S(1)}, s32[4,64]{1,0:T(4,128)}, u32[]{:S(2)}) copy-start(s32[4,64]{1,0:T(4,128)} %param.7) | copy-start | bytes 3076
  2.3 36.2 %all-to-all-start = ((f32[2,256,256]{2,0,1:T(2,128)}), f32[2,256,256]{2,0,1:T(2,128)S(1)}, u32[]{:S(2)}, u32[]{:S(2)}) async-start(f32[2,256,256]{2,0,1:T(2,128)} %copy.22), calls=%async_computation | async-start | bytes 1048576 | tf_op jit(solution)/shard_map/all_to_all | solution.py:113
  19.2 0.7 %copy-start = (f32[3,256]{1,0:T(4,128)S(1)}, f32[3,256]{1,0:T(4,128)}, u32[]{:S(2)}) copy-start(f32[3,256]{1,0:T(4,128)} %param.5) | copy-start | bytes 9220
  19.9 0.7 %copy-start.1 = (f32[256]{0:T(256)S(1)}, f32[256]{0:T(256)}, u32[]{:S(2)}) copy-start(f32[256]{0:T(256)} %param.6) | copy-start | bytes 3076

commit v2 on v1

--- a/solution.py
+++ b/solution.py
@@ -101,6 +101,56 @@
     return layers[:, 0]
 
 
+def exchange_kernel(send_ref, out_ref, landed, send_sem, recv_sem, own_sem):
+    devices = send_ref.shape[0]
+    members = lax.axis_size("tile")
+    me = lax.axis_index("grp") * members + lax.axis_index("tile")
+
+    def send(k, carry):
+        dest = lax.rem(me + k, devices)
+        pltpu.make_async_remote_copy(
+            src_ref=send_ref.at[pl.ds(dest, 1)],
+            dst_ref=landed.at[pl.ds(me, 1)],
+            send_sem=send_sem,
+            recv_sem=recv_sem,
+            device_id=(dest // members, dest % members),
+            device_id_type=pl.DeviceIdType.MESH,
+        ).start()
+        return carry
+
+    lax.fori_loop(1, devices, send, 0)
+    own = pltpu.make_async_copy(send_ref.at[pl.ds(me, 1)], landed.at[pl.ds(me, 1)], own_sem)
+    own.start()
+    own.wait()
+    everything = pltpu.make_async_remote_copy(
+        src_ref=send_ref.at[pl.ds(0, devices - 1)],
+        dst_ref=landed.at[pl.ds(0, devices - 1)],
+        send_sem=send_sem,
+        recv_sem=recv_sem,
+        device_id=(me // members, me % members),
+        device_id_type=pl.DeviceIdType.MESH,
+    )
+    everything.wait_send()
+    everything.wait_recv()
+    out_ref[...] = landed[...]
+
+
+def exchange(rows):
+    return pl.pallas_call(
+        exchange_kernel,
+        out_shape=jax.ShapeDtypeStruct(rows.shape, rows.dtype),
+        in_specs=[pl.BlockSpec(memory_space=pltpu.VMEM)],
+        out_specs=pl.BlockSpec(memory_space=pltpu.VMEM),
+        scratch_shapes=[
+            pltpu.VMEM(rows.shape, rows.dtype),
+            pltpu.SemaphoreType.DMA,
+            pltpu.SemaphoreType.DMA,
+            pltpu.SemaphoreType.DMA,
+        ],
+        compiler_params=pltpu.CompilerParams(has_side_effects=True),
+    )(rows)
+
+
 def body(bricks, colour_table, opacity_table, depth_order):
     palette = jnp.concatenate([colour_table, opacity_table[None, :]], axis=0)
     groups = lax.axis_size("grp")
@@ -109,8 +159,10 @@
     depth = bricks.shape[0]
     pixels = bricks.shape[1] * bricks.shape[2]
     block = pixels // devices
-    local = bricks.reshape(depth, devices, block)
-    gathered = lax.all_to_all(local, ("grp", "tile"), 1, 1, tiled=True)
+    rows = jnp.transpose(bricks.reshape(depth, devices, block), (1, 0, 2))
+    rows = rows.reshape(devices, depth * block // LANES, LANES)
+    arrived = exchange(rows)
+    gathered = jnp.transpose(arrived.reshape(devices, depth, block), (1, 0, 2))
     partials = shade_bricks(gathered, palette)
     by_rank = jnp.argsort(depth_order, axis=1).astype(jnp.int32)
     sequence = (jnp.arange(groups, dtype=jnp.int32)[:, None] * members + by_rank).reshape(-1)

time: 52.8 us -> 58.8 us (1.11)
  Pallas kernels: 7.26 us -> 44 us
  waiting for transfers between devices: 17.8 us -> 0 us
  starting transfers between devices: 15.6 us -> 0 us
  local copies, waits for them, and re-layouts: 8.67 us -> 11.4 us
    pallas_call x0 -> x1, Pallas kernels: none -> 36.7 us  [exchange(): pl.pallas_call(exchange_kernel, out_shape=jax.ShapeDtypeStruct(rows.shape...]
    all_to_all x1 -> x0, waiting for transfers between devices: 17.8 us -> none  [body(): gathered = lax.all_to_all(local, ('grp', 'tile'), 1, 1, tiled=True)]
    all_to_all x1 -> x0, starting transfers between devices: 15.6 us -> none  [body(): gathered = lax.all_to_all(local, ('grp', 'tile'), 1, 1, tiled=True)]
    reshape x2 -> x4, local copies, waits for them, and re-layouts: 2.33 us -> 3.86 us  [the longest x2 1.54 us: body(): rows = jnp.transpose(bricks.reshape(depth, devices, block), (1, 0, 2))]
    pallas_call x0 -> x1, local copies, waits for them, and re-layouts: none -> 1.24 us  [exchange(): pl.pallas_call(exchange_kernel, out_shape=jax.ShapeDtypeStruct(rows.shape...]
    all_to_all x1 -> x0, local copies, waits for them, and re-layouts: 0.86 us -> none  [body(): gathered = lax.all_to_all(local, ('grp', 'tile'), 1, 1, tiled=True)]
    unnamed x14, local copies, waits for them, and re-layouts: 1.34 us -> 2.14 us
  transfers between devices with their start and end apart: 1 -> 0, of which waited for: 1 -> 0; matrix products, arithmetic and copies ran while one was open for 3% -> 0% of each run, Pallas kernels for 0% -> 0%
where the time goes in v2:
time: 58.8 us; the launch traced here: 58.5 us
  Pallas kernels  44 us (75%)
  local copies, waits for them, and re-layouts  11.4 us (19%)
  other arithmetic  2.82 us (5%)
    pallas_call x1, Pallas kernels, exchange(): pl.pallas_call(exchange_kernel, out_shape=jax.ShapeDtypeStruct(rows.shape...  36.7 us
    pallas_call x1, Pallas kernels, shade_bricks(): pl.pallas_call(kernel, out_shape=jax.ShapeDtypeStruct((channels, bricks,...  7.26 us
    unnamed x14, local copies, waits for them, and re-layouts  2.14 us
    pallas_call x1, local copies, waits for them, and re-layouts, shade_bricks(): pl.pallas_call(kernel, out_shape=jax.ShapeDtypeStruct((channels, bricks,...  1.9 us
    reshape x2, local copies, waits for them, and re-layouts, body(): rows = jnp.transpose(bricks.reshape(depth, devices, block), (1, 0, 2))  1.54 us
    reshape x1, local copies, waits for them, and re-layouts, body(): rows = rows.reshape(devices, depth * block // LANES, LANES)  1.3 us
    gather x1, local copies, waits for them, and re-layouts, body(): ordered = jnp.take(partials, sequence, axis=1)  1.27 us
    pallas_call x1, local copies, waits for them, and re-layouts, exchange(): pl.pallas_call(exchange_kernel, out_shape=jax.ShapeDtypeStruct(rows.shape...  1.24 us

profile of v2, /device:TPU:1, one launch (start us, length us, event | category | flops | bytes accessed | tf_op | source)
XLA Modules:
  0.0 58.5 jit_solution(8043729260166402591)
XLA Ops:
  0.0 0.0 copy-start
  0.0 0.7 %copy-done = f32[3,256]{1,0:T(4,128)S(1)} copy-done((f32[3,256]{1,0:T(4,128)S(1)}, f32[3,256]{1,0:T(4,128)}, u32[]{:S(2)}) %copy-start) | copy-done | bytes 3096
  0.7 0.0 copy-start.1
  0.7 0.7 %copy-done.1 = f32[256]{0:T(256)S(1)} copy-done((f32[256]{0:T(256)S(1)}, f32[256]{0:T(256)}, u32[]{:S(2)}) %copy-start.1) | copy-done | bytes 1048
  1.4 0.1 fusion.2
  1.5 0.0 copy-start.2
  1.5 0.7 %copy-done.2 = s32[4,64]{1,0:T(4,128)S(1)} copy-done((s32[4,64]{1,0:T(4,128)S(1)}, s32[4,64]{1,0:T(4,128)}, u32[]{:S(2)}) %copy-start.2) | copy-done | bytes 1048
  2.2 0.1 copy.13
  2.3 1.0 %sort.17 = (s32[4,64]{0,1:T(8,128)}, s32[4,64]{0,1:T(8,128)S(1)}) sort(s32[4,64]{0,1:T(8,128)S(1)} %copy.13, s32[4,64]{0,1:T(8,128)S(1)} %iota.13), dimensions={1}, to_apply=%region_0.0 | sort | flops 2048 | bytes 4096 | tf_op jit(solution)/shard_map/jit(argsort)/sort | solution.py:167
  3.3 0.1 copy.14
  3.3 0.1 reshape.66
  3.4 0.1 reshape.62
  3.5 0.6 %broadcast_in_dim.25.tables_ref = f32[16,8,128]{2,1,0:T(8,128)} broadcast(f32[16,128]{1,0:T(8,128)S(1)} %bitcast.42), dimensions={0,2} | broadcast | bytes 73728 | tf_op jit(solution)/shard_map/broadcast_in_dim | solution.py:19
  4.2 1.1 %reshape.63 = f32[2,256,256]{2,1,0:T(8,128)S(1)} reshape(f32[2,128,512]{2,1,0:T(8,128)} %param.4) | data formatting | bytes 1048576 | tf_op jit(solution)/shard_map/reshape | solution.py:162
  5.3 0.4 copy.36
  5.7 1.3 %reshape.64.send_ref = f32[256,4,128]{2,1,0:T(4,128)} reshape(f32[256,2,256]{2,1,0:T(2,128)S(1)} %bitcast.36) | data formatting | bytes 1048576 | tf_op jit(solution)/shard_map/reshape | solution.py:163
  7.0 36.7 %shard_map.46 = f32[256,4,128]{2,1,0:T(4,128)} custom-call(f32[256,4,128]{2,1,0:T(4,128)} %reshape.64.send_ref), custom_call_target="tpu_custom_call" | custom-call | tf_op jit(solution)/shard_map/pallas_call | solution.py:139
  43.8 1.2 %copy.16 = f32[256,4,128]{0,2,1:T(8,128)S(1)} copy(f32[256,4,128]{2,1,0:T(4,128)} %shard_map.46) | data formatting | bytes 1048576 | tf_op jit(solution)/shard_map/pallas_call | solution.py:139
  45.0 1.0 %copy.17 = f32[256,2,256]{2,0,1:T(8,128)} copy(f32[256,2,256]{0,2,1:T(8,128)S(1)} %bitcast.37) | data formatting | bytes 1048576 | tf_op jit(solution)/shard_map/reshape | solution.py:165
  46.0 7.3 %shard_map.47 = f32[4,256,256]{2,1,0:T(8,128)} custom-call(f32[2,256,256]{2,1,0:T(8,128)} %bitcast.35, f32[16,8,128]{2,1,0:T(8,128)} %broadcast_in_dim.25.tables_ref), custom_call_target="tpu_custom_call" | custom-call | tf_op jit(solution)/shard_map/pallas_call | solution.py:85
  53.3 1.9 %copy.20 = f32[4,256,256]{2,0,1:T(4,128)S(1)} copy(f32[4,256,256]{2,1,0:T(8,128)} %shard_map.47) | data formatting | bytes 2097152 | tf_op jit(solution)/shard_map/pallas_call | solution.py:85
  55.2 1.3 %gather_fusion = f32[256,4,256]{2,1,0:T(4,128)S(1)} fusion(f32[4,256,256]{2,0,1:T(4,128)S(1)} %copy.20, s32[1024]{0:T(1024)S(1)} %pad_clamp_fusion), kind=kCustom, calls=%fused_computation | custom fusion | bytes 2098176 | tf_op jit(solution)/shard_map/jit(_take)/gather | solution.py:169
  56.5 0.3 select_bitcast_fusion
  56.8 0.2 slice_subtract_fusion
  57.0 0.2 multiply_add_fusion
  57.3 0.1 slice_subtract_fusion.1
  57.4 0.1 multiply_add_fusion.1
  57.9 0.6 %fusion.1 = f32[4,256]{1,0:T(4,128)} fusion(f32[4,2,256]{2,0,1:T(4,128)S(1)} %multiply_add_fusion.6, f32[256]{0:T(256)S(1)} %bitcast.49), kind=kLoop, calls=%fused_computation.25 | loop fusion | flops 2048 | bytes 13312 | tf_op jit(solution)/shard_map/squeeze | solution.py:101
  (35 shorter events, 0.4 us)
Async XLA Ops:
  0.0 0.7 %copy-start = (f32[3,256]{1,0:T(4,128)S(1)}, f32[3,256]{1,0:T(4,128)}, u32[]{:S(2)}) copy-start(f32[3,256]{1,0:T(4,128)} %param.5) | copy-start | bytes 9220
  0.7 0.7 %copy-start.1 = (f32[256]{0:T(256)S(1)}, f32[256]{0:T(256)}, u32[]{:S(2)}) copy-start(f32[256]{0:T(256)} %param.6) | copy-start | bytes 3076
  1.5 0.7 %copy-start.2 = (s32[4,64]{1,0:T(4,128)S(1)}, s32[4,64]{1,0:T(4,128)}, u32[]{:S(2)}) copy-start(s32[4,64]{1,0:T(4,128)} %param.7) | copy-start | bytes 3076

commit v3 on v2

v3 whole, which is shorter than its diff:
```python
import functools

import jax
import jax.numpy as jnp
from jax import lax
from jax.experimental import pallas as pl
from jax.experimental.pallas import tpu as pltpu
from jax.sharding import PartitionSpec as P

LANES = 128


def render_kernel(members, values_ref, colour_ref, opacity_ref, order_ref, out_ref, parts_ref):
    tiles, sub, lanes = values_ref.shape
    knots = colour_ref.shape[1]
    halves = knots // lanes
    colours = colour_ref.shape[0]
    groups = parts_ref.shape[1] // members
    rows = [colour_ref[c : c + 1, :] for c in range(colours)] + [opacity_ref[...]]
    tables = [
        [jnp.broadcast_to(r[:, h * lanes : (h + 1) * lanes], (sub, lanes)) for h in range(halves)]
        for r in rows
    ]

    def pick(c, index):
        lane = index % lanes
        half = index // lanes
        got = jnp.take_along_axis(tables[c][0], lane, axis=1, mode="promise_in_bounds")
        for h in range(1, halves):
            other = jnp.take_along_axis(tables[c][h], lane, axis=1, mode="promise_in_bounds")
            got = jnp.where(half == h, other, got)
        return got

    def sample(v):
        u = v * float(knots - 1)
        lower = jnp.clip(jnp.floor(u), 0.0, float(knots - 2))
        frac = u - lower
        index = lower.astype(jnp.int32)
        return [pick(c, index) * (1.0 - frac) + pick(c, index + 1) * frac for c in range(colours + 1)]

    def shade(m, carry):
        front = sample(values_ref[m])
        back = [pltpu.roll(x, sub - 2, 0) for x in front]
        a0 = front[colours]
        a1 = back[colours]
        colour = [a0 * front[c] for c in range(colours)]
        transmit = 1.0 - a0
        weight = transmit * a1
        colour = [colour[c] + weight * back[c] for c in range(colours)]
        transmit = transmit * (1.0 - a1)
        part = colour + [1.0 - transmit]
        for e in range(2):
            brick = 2 * m + e
            place = (brick // members) * members + order_ref[brick]
            for c in range(colours + 1):
                parts_ref[c, place] = part[c][4 * e : 4 * e + 2]
        return carry

    lax.fori_loop(0, tiles, shade, 0)

    def blend(k, pics):
        out = []
        for g in range(groups):
            pic = pics[g]
            clear = 1.0 - pic[colours]
            out.append(tuple(pic[c] + clear * parts_ref[c, g * members + k] for c in range(colours + 1)))
        return tuple(out)

    zero = jnp.zeros((2, lanes), jnp.float32)
    pics = lax.fori_loop(0, members, blend, tuple(tuple(zero for _ in range(colours + 1)) for _ in range(groups)))
    final = pics[0]
    for g in range(1, groups):
        clear = 1.0 - final[colours]
        final = tuple(final[c] + clear * pics[g][c] for c in range(colours + 1))
    for c in range(colours + 1):
        out_ref[c] = final[c]


def render(arrived, colour_table, opacity_table, depth_order):
    devices = arrived.shape[0]
    groups, members = depth_order.shape
    lanes = arrived.shape[2]
    tiles = arrived.reshape(devices // 2, 2 * arrived.shape[1], lanes)
    channels = colour_table.shape[0] + 1
    vmem = pl.BlockSpec(memory_space=pltpu.VMEM)
    picture = pl.pallas_call(
        functools.partial(render_kernel, members),
        out_shape=jax.ShapeDtypeStruct((channels, 2, lanes), jnp.float32),
        in_specs=[vmem, vmem, vmem, pl.BlockSpec(memory_space=pltpu.SMEM)],
        out_specs=vmem,
        scratch_shapes=[pltpu.VMEM((channels, devices, 2, lanes), jnp.float32)],
    )(tiles, colour_table, opacity_table.reshape(1, -1), depth_order.reshape(-1))
    return picture.reshape(channels, 2 * lanes)


def exchange_kernel(send_ref, out_ref, landed, send_sem, recv_sem, own_sem):
    devices = send_ref.shape[0]
    members = lax.axis_size("tile")
    me = lax.axis_index("grp") * members + lax.axis_index("tile")

    def send(k, carry):
        dest = lax.rem(me + k, devices)
        pltpu.make_async_remote_copy(
            src_ref=send_ref.at[pl.ds(dest, 1)],
            dst_ref=landed.at[pl.ds(me, 1)],
            send_sem=send_sem,
            recv_sem=recv_sem,
            device_id=(dest // members, dest % members),
            device_id_type=pl.DeviceIdType.MESH,
        ).start()
        return carry

    lax.fori_loop(1, devices, send, 0)
    own = pltpu.make_async_copy(send_ref.at[pl.ds(me, 1)], landed.at[pl.ds(me, 1)], own_sem)
    own.start()
    own.wait()
    everything = pltpu.make_async_remote_copy(
        src_ref=send_ref.at[pl.ds(0, devices - 1)],
        dst_ref=landed.at[pl.ds(0, devices - 1)],
        send_sem=send_sem,
        recv_sem=recv_sem,
        device_id=(me // members, me % members),
        device_id_type=pl.DeviceIdType.MESH,
    )
    everything.wait_send()
    everything.wait_recv()
    out_ref[...] = landed[...]


def exchange(rows):
    return pl.pallas_call(
        exchange_kernel,
        out_shape=jax.ShapeDtypeStruct(rows.shape, rows.dtype),
        in_specs=[pl.BlockSpec(memory_space=pltpu.VMEM)],
        out_specs=pl.BlockSpec(memory_space=pltpu.VMEM),
        scratch_shapes=[
            pltpu.VMEM(rows.shape, rows.dtype),
            pltpu.SemaphoreType.DMA,
            pltpu.SemaphoreType.DMA,
            pltpu.SemaphoreType.DMA,
        ],
        compiler_params=pltpu.CompilerParams(has_side_effects=True),
    )(rows)


def body(bricks, colour_table, opacity_table, depth_order):
    groups = lax.axis_size("grp")
    members = lax.axis_size("tile")
    devices = groups * members
    depth = bricks.shape[0]
    pixels = bricks.shape[1] * bricks.shape[2]
    block = pixels // devices
    rows = jnp.transpose(bricks.reshape(depth, devices, block), (1, 0, 2))
    rows = rows.reshape(devices, depth * block // LANES, LANES)
    arrived = exchange(rows)
    return render(arrived, colour_table, opacity_table, depth_order)


def solution(mesh):
    in_specs = (P(("grp", "tile"), None, None), P(), P(), P())
    out_specs = P(None, ("grp", "tile"))
    return jax.shard_map(body, mesh=mesh, in_specs=in_specs, out_specs=out_specs, check_vma=False)
```

time: 58.8 us -> 58.4 us (level)
  Pallas kernels: 44 us -> 53.4 us
  local copies, waits for them, and re-layouts: 11.4 us -> 4.77 us
  other arithmetic: 2.82 us -> 0 us
    pallas_call x1, Pallas kernels: 7.26 us -> 16.7 us  [render(): pl.pallas_call(functools.partial(render_kernel, members), out_shape=jax.S...]
    pallas_call x2 -> x0, local copies, waits for them, and re-layouts: 3.14 us -> none  [the longest x1 1.9 us: shade_bricks(): pl.pallas_call(kernel, out_shape=jax.ShapeDtypeStruct((channels, bricks,...]
    gather x1 -> x0, local copies, waits for them, and re-layouts: 1.27 us -> none  [body(): ordered = jnp.take(partials, sequence, axis=1)]
    sort x1 -> x0, other arithmetic: 1.01 us -> none  [body(): by_rank = jnp.argsort(depth_order, axis=1).astype(jnp.int32)]
    unnamed x14 -> x3, local copies, waits for them, and re-layouts: 2.14 us -> 1.27 us
    broadcast_in_dim x1 -> x0, local copies, waits for them, and re-layouts: 0.62 us -> none  [lookup_tables(): jnp.broadcast_to(tables[..., None, :], (channels, 2, halves, ROWS_PER_STE...]
    squeeze x1 -> x0, other arithmetic: 0.6 us -> none  [composite(): return layers[:, 0]]
    reshape x3 -> x1, local copies, waits for them, and re-layouts: 1.19 us -> 0.64 us  [render(): depth_order.reshape(-1)]
where the time goes in v3:
time: 58.4 us; the launch traced here: 58.2 us
  Pallas kernels  53.4 us (91%)
  local copies, waits for them, and re-layouts  4.77 us (8%)
    pallas_call x1, Pallas kernels, exchange(): pl.pallas_call(exchange_kernel, out_shape=jax.ShapeDtypeStruct(rows.shape...  36.7 us
    pallas_call x1, Pallas kernels, render(): pl.pallas_call(functools.partial(render_kernel, members), out_shape=jax.S...  16.7 us
    reshape x2, local copies, waits for them, and re-layouts, body(): rows = jnp.transpose(bricks.reshape(depth, devices, block), (1, 0, 2))  1.54 us
    reshape x1, local copies, waits for them, and re-layouts, body(): rows = rows.reshape(devices, depth * block // LANES, LANES)  1.32 us
    unnamed x3, local copies, waits for them, and re-layouts  1.27 us

profile of v3, /device:TPU:1, one launch (start us, length us, event | category | flops | bytes accessed | tf_op | source)
XLA Modules:
  0.0 58.2 jit_solution(475667295794297485)
XLA Ops:
  0.0 1.1 %reshape.18 = f32[2,256,256]{2,1,0:T(8,128)S(1)} reshape(f32[2,128,512]{2,1,0:T(8,128)} %param.4) | data formatting | bytes 1048576 | tf_op jit(solution)/shard_map/reshape | solution.py:153
  1.1 0.4 copy.9
  1.5 1.3 %reshape.19.send_ref = f32[256,4,128]{2,1,0:T(4,128)} reshape(f32[256,2,256]{2,1,0:T(2,128)S(1)} %bitcast.10) | data formatting | bytes 1048576 | tf_op jit(solution)/shard_map/reshape | solution.py:154
  2.9 0.0 copy-start
  2.9 36.7 %shard_map.46 = f32[256,4,128]{2,1,0:T(4,128)} custom-call(f32[256,4,128]{2,1,0:T(4,128)} %reshape.19.send_ref), custom_call_target="tpu_custom_call" | custom-call | tf_op jit(solution)/shard_map/pallas_call | solution.py:131
  39.6 0.0 copy-done
  39.6 0.6 %reshape.22.order_ref = s32[256]{0:T(256)} reshape(s32[4,64]{1,0:T(4,128)S(1)} %copy-done) | data formatting | bytes 2048 | tf_op jit(solution)/shard_map/reshape | solution.py:92
  40.2 16.7 %shard_map.47 = f32[4,2,128]{2,1,0:T(2,128)} custom-call(f32[128,8,128]{2,1,0:T(8,128)} %bitcast.9, f32[3,256]{1,0:T(4,128)} %colour_ref.1, f32[1,256]{1,0:T(1,128)} %bitcast.12, s32[256]{0:T(256)} %reshape.22.order_ref), custom_call_target="tpu_custom_call" | custom-call | tf_op jit(solution)/shard_map/pallas_call | solution.py:86
  56.9 1.3 %copy.10 = f32[1,4,2,128]{3,1,2,0:T(4,128)} copy(f32[1,4,2,128]{3,2,1,0:T(2,128)} %bitcast.11) | data formatting | bytes 8192
Async XLA Ops:
  2.9 36.7 %copy-start = (s32[4,64]{1,0:T(4,128)S(1)}, s32[4,64]{1,0:T(4,128)}, u32[]{:S(2)}) copy-start(s32[4,64]{1,0:T(4,128)} %param.7) | copy-start | bytes 3076

commit v4 on v3

--- a/solution.py
+++ b/solution.py
@@ -51,12 +51,12 @@
         part = colour + [1.0 - transmit]
         for e in range(2):
             brick = 2 * m + e
-            place = (brick // members) * members + order_ref[brick]
+            place = (brick // members) * members + order_ref[brick // members, brick % members]
             for c in range(colours + 1):
-                parts_ref[c, place] = part[c][4 * e : 4 * e + 2]
+                parts_ref[c, place] = part[c] if e == 0 else pltpu.roll(part[c], sub - 4, 0)
         return carry
 
-    lax.fori_loop(0, tiles, shade, 0)
+    lax.fori_loop(0, tiles, shade, 0, unroll=2)
 
     def blend(k, pics):
         out = []
@@ -66,31 +66,33 @@
             out.append(tuple(pic[c] + clear * parts_ref[c, g * members + k] for c in range(colours + 1)))
         return tuple(out)
 
-    zero = jnp.zeros((2, lanes), jnp.float32)
-    pics = lax.fori_loop(0, members, blend, tuple(tuple(zero for _ in range(colours + 1)) for _ in range(groups)))
+    zero = jnp.zeros((sub, lanes), jnp.float32)
+    start = tuple(tuple(zero for _ in range(colours + 1)) for _ in range(groups))
+    pics = lax.fori_loop(0, members, blend, start, unroll=4)
     final = pics[0]
     for g in range(1, groups):
         clear = 1.0 - final[colours]
         final = tuple(final[c] + clear * pics[g][c] for c in range(colours + 1))
     for c in range(colours + 1):
-        out_ref[c] = final[c]
+        for j in range(2):
+            out_ref[c : c + 1, j * lanes : (j + 1) * lanes] = final[c][j : j + 1]
 
 
 def render(arrived, colour_table, opacity_table, depth_order):
     devices = arrived.shape[0]
     groups, members = depth_order.shape
     lanes = arrived.shape[2]
-    tiles = arrived.reshape(devices // 2, 2 * arrived.shape[1], lanes)
+    sub = 2 * arrived.shape[1]
+    tiles = arrived.reshape(devices // 2, sub, lanes)
     channels = colour_table.shape[0] + 1
     vmem = pl.BlockSpec(memory_space=pltpu.VMEM)
-    picture = pl.pallas_call(
+    return pl.pallas_call(
         functools.partial(render_kernel, members),
-        out_shape=jax.ShapeDtypeStruct((channels, 2, lanes), jnp.float32),
+        out_shape=jax.ShapeDtypeStruct((channels, 2 * lanes), jnp.float32),
         in_specs=[vmem, vmem, vmem, pl.BlockSpec(memory_space=pltpu.SMEM)],
         out_specs=vmem,
-        scratch_shapes=[pltpu.VMEM((channels, devices, 2, lanes), jnp.float32)],
-    )(tiles, colour_table, opacity_table.reshape(1, -1), depth_order.reshape(-1))
-    return picture.reshape(channels, 2 * lanes)
+        scratch_shapes=[pltpu.VMEM((channels, devices, sub, lanes), jnp.float32)],
+    )(tiles, colour_table, opacity_table.reshape(1, -1), depth_order)
 
 
 def exchange_kernel(send_ref, out_ref, landed, send_sem, recv_sem, own_sem):

time: 58.4 us -> 51.4 us (0.88)
  Pallas kernels: 53.4 us -> 48.3 us
  local copies, waits for them, and re-layouts: 4.77 us -> 2.84 us
    pallas_call x1, Pallas kernels: 16.7 us -> 11.6 us  [render(): pl.pallas_call(functools.partial(render_kernel, members), out_shape=jax.S...]
    unnamed x3 -> x0, local copies, waits for them, and re-layouts: 1.27 us -> none
    reshape x1 -> x0, local copies, waits for them, and re-layouts: 0.64 us -> none  [render(): depth_order.reshape(-1)]
where the time goes in v4:
time: 51.4 us; the launch traced here: 51.2 us
  Pallas kernels  48.3 us (94%)
  local copies, waits for them, and re-layouts  2.84 us (6%)
    pallas_call x1, Pallas kernels, exchange(): pl.pallas_call(exchange_kernel, out_shape=jax.ShapeDtypeStruct(rows.shape...  36.7 us
    pallas_call x1, Pallas kernels, render(): pl.pallas_call(functools.partial(render_kernel, members), out_shape=jax.S...  11.6 us
    reshape x2, local copies, waits for them, and re-layouts, body(): rows = jnp.transpose(bricks.reshape(depth, devices, block), (1, 0, 2))  1.54 us
    reshape x1, local copies, waits for them, and re-layouts, body(): rows = rows.reshape(devices, depth * block // LANES, LANES)  1.3 us

profile of v4, /device:TPU:1, one launch (start us, length us, event | category | flops | bytes accessed | tf_op | source)
XLA Modules:
  0.0 51.2 jit_solution(10654900977239574707)
XLA Ops:
  0.0 1.1 %reshape.12 = f32[2,256,256]{2,1,0:T(8,128)S(1)} reshape(f32[2,128,512]{2,1,0:T(8,128)} %param.4) | data formatting | bytes 1048576 | tf_op jit(solution)/shard_map/reshape | solution.py:155
  1.1 0.4 copy.7
  1.5 1.3 %reshape.13.send_ref = f32[256,4,128]{2,1,0:T(4,128)} reshape(f32[256,2,256]{2,1,0:T(2,128)S(1)} %bitcast.5) | data formatting | bytes 1048576 | tf_op jit(solution)/shard_map/reshape | solution.py:156
  2.8 36.7 %shard_map.46 = f32[256,4,128]{2,1,0:T(4,128)} custom-call(f32[256,4,128]{2,1,0:T(4,128)} %reshape.13.send_ref), custom_call_target="tpu_custom_call" | custom-call | tf_op jit(solution)/shard_map/pallas_call | solution.py:133
  39.6 11.6 %shard_map.47 = f32[4,256]{1,0:T(4,128)} custom-call(f32[128,8,128]{2,1,0:T(8,128)} %bitcast.6, f32[3,256]{1,0:T(4,128)} %colour_ref.1, f32[1,256]{1,0:T(1,128)} %bitcast.7, s32[4,64]{1,0:T(4,128)} %order_ref.1), custom_call_target="tpu_custom_call" | custom-call | tf_op jit(solution)/shard_map/pallas_call | solution.py:89

commit v5 on v4

--- a/solution.py
+++ b/solution.py
@@ -1,4 +1,5 @@
 import functools
+import math
 
 import jax
 import jax.numpy as jnp
@@ -95,13 +96,22 @@
     )(tiles, colour_table, opacity_table.reshape(1, -1), depth_order)
 
 
+def spread_stride(devices):
+    step = (3 * devices) // 8 + 1
+    while math.gcd(step, devices) != 1:
+        step += 1
+    return step
+
+
 def exchange_kernel(send_ref, out_ref, landed, send_sem, recv_sem, own_sem):
     devices = send_ref.shape[0]
     members = lax.axis_size("tile")
     me = lax.axis_index("grp") * members + lax.axis_index("tile")
 
+    stride = spread_stride(devices)
+
     def send(k, carry):
-        dest = lax.rem(me + k, devices)
+        dest = lax.rem(me + k * stride, devices)
         pltpu.make_async_remote_copy(
             src_ref=send_ref.at[pl.ds(dest, 1)],
             dst_ref=landed.at[pl.ds(me, 1)],

time: 51.4 us -> 53.2 us (1.035)
  Pallas kernels: 48.3 us -> 50.2 us
    pallas_call x1, Pallas kernels: 36.7 us -> 38.6 us  [exchange(): pl.pallas_call(exchange_kernel, out_shape=jax.ShapeDtypeStruct(rows.shape...]
where the time goes in v5:
time: 53.2 us; the launch traced here: 53 us
  Pallas kernels  50.2 us (94%)
  local copies, waits for them, and re-layouts  2.84 us (5%)
    pallas_call x1, Pallas kernels, exchange(): pl.pallas_call(exchange_kernel, out_shape=jax.ShapeDtypeStruct(rows.shape...  38.6 us
    pallas_call x1, Pallas kernels, render(): pl.pallas_call(functools.partial(render_kernel, members), out_shape=jax.S...  11.6 us
    reshape x2, local copies, waits for them, and re-layouts, body(): rows = jnp.transpose(bricks.reshape(depth, devices, block), (1, 0, 2))  1.54 us
    reshape x1, local copies, waits for them, and re-layouts, body(): rows = rows.reshape(devices, depth * block // LANES, LANES)  1.3 us

profile of v5, /device:TPU:1, one launch (start us, length us, event | category | flops | bytes accessed | tf_op | source)
XLA Modules:
  0.0 53.0 jit_solution(14282482082816301717)
XLA Ops:
  0.0 1.1 %reshape.12 = f32[2,256,256]{2,1,0:T(8,128)S(1)} reshape(f32[2,128,512]{2,1,0:T(8,128)} %param.4) | data formatting | bytes 1048576 | tf_op jit(solution)/shard_map/reshape | solution.py:165
  1.1 0.4 copy.7
  1.5 1.3 %reshape.13.send_ref = f32[256,4,128]{2,1,0:T(4,128)} reshape(f32[256,2,256]{2,1,0:T(2,128)S(1)} %bitcast.5) | data formatting | bytes 1048576 | tf_op jit(solution)/shard_map/reshape | solution.py:166
  2.8 38.6 %shard_map.46 = f32[256,4,128]{2,1,0:T(4,128)} custom-call(f32[256,4,128]{2,1,0:T(4,128)} %reshape.13.send_ref), custom_call_target="tpu_custom_call" | custom-call | tf_op jit(solution)/shard_map/pallas_call | solution.py:143
  41.4 11.6 %shard_map.47 = f32[4,256]{1,0:T(4,128)} custom-call(f32[128,8,128]{2,1,0:T(8,128)} %bitcast.6, f32[3,256]{1,0:T(4,128)} %colour_ref.1, f32[1,256]{1,0:T(1,128)} %bitcast.7, s32[4,64]{1,0:T(4,128)} %order_ref.1), custom_call_target="tpu_custom_call" | custom-call | tf_op jit(solution)/shard_map/pallas_call | solution.py:90

commit v6 on v4

v6 whole, which is shorter than its diff:
```python
import functools

import jax
import jax.numpy as jnp
from jax import lax
from jax.experimental import pallas as pl
from jax.experimental.pallas import tpu as pltpu
from jax.sharding import PartitionSpec as P

LANES = 128


def make_sampler(colour_ref, opacity_ref, sub):
    knots = colour_ref.shape[1]
    lanes = LANES
    halves = knots // lanes
    colours = colour_ref.shape[0]
    rows = [colour_ref[c : c + 1, :] for c in range(colours)] + [opacity_ref[...]]
    tables = [
        [jnp.broadcast_to(r[:, h * lanes : (h + 1) * lanes], (sub, lanes)) for h in range(halves)]
        for r in rows
    ]

    def pick(c, index):
        lane = index % lanes
        half = index // lanes
        got = jnp.take_along_axis(tables[c][0], lane, axis=1, mode="promise_in_bounds")
        for h in range(1, halves):
            other = jnp.take_along_axis(tables[c][h], lane, axis=1, mode="promise_in_bounds")
            got = jnp.where(half == h, other, got)
        return got

    def sample(v):
        u = v * float(knots - 1)
        lower = jnp.clip(jnp.floor(u), 0.0, float(knots - 2))
        frac = u - lower
        index = lower.astype(jnp.int32)
        return [pick(c, index) * (1.0 - frac) + pick(c, index + 1) * frac for c in range(colours + 1)]

    return sample


def shade_tile(sample, v):
    sub = v.shape[0]
    front = sample(v)
    colours = len(front) - 1
    back = [pltpu.roll(x, sub - 2, 0) for x in front]
    a0 = front[colours]
    a1 = back[colours]
    colour = [a0 * front[c] for c in range(colours)]
    transmit = 1.0 - a0
    weight = transmit * a1
    colour = [colour[c] + weight * back[c] for c in range(colours)]
    transmit = transmit * (1.0 - a1)
    return colour + [1.0 - transmit]


def composite_kernel(members, partial_ref, order_ref, out_ref, parts_ref):
    channels, tiles, sub, lanes = partial_ref.shape
    colours = channels - 1
    groups = parts_ref.shape[1] // members

    def scatter(m, carry):
        for e in range(2):
            brick = 2 * m + e
            place = (brick // members) * members + order_ref[brick // members, brick % members]
            for c in range(channels):
                part = partial_ref[c, m]
                parts_ref[c, place] = part if e == 0 else pltpu.roll(part, sub - 4, 0)
        return carry

    lax.fori_loop(0, tiles, scatter, 0, unroll=2)

    def blend(k, pics):
        out = []
        for g in range(groups):
            pic = pics[g]
            clear = 1.0 - pic[colours]
            out.append(tuple(pic[c] + clear * parts_ref[c, g * members + k] for c in range(channels)))
        return tuple(out)

    zero = jnp.zeros((sub, lanes), jnp.float32)
    start = tuple(tuple(zero for _ in range(channels)) for _ in range(groups))
    pics = lax.fori_loop(0, members, blend, start, unroll=4)
    final = pics[0]
    for g in range(1, groups):
        clear = 1.0 - final[colours]
        final = tuple(final[c] + clear * pics[g][c] for c in range(channels))
    for c in range(channels):
        for j in range(2):
            out_ref[c : c + 1, j * lanes : (j + 1) * lanes] = final[c][j : j + 1]


def composite(partials, depth_order):
    channels, tiles, sub, lanes = partials.shape
    groups, members = depth_order.shape
    vmem = pl.BlockSpec(memory_space=pltpu.VMEM)
    return pl.pallas_call(
        functools.partial(composite_kernel, members),
        out_shape=jax.ShapeDtypeStruct((channels, 2 * lanes), jnp.float32),
        in_specs=[vmem, pl.BlockSpec(memory_space=pltpu.SMEM)],
        out_specs=vmem,
        scratch_shapes=[pltpu.VMEM((channels, 2 * tiles, sub, lanes), jnp.float32)],
    )(partials, depth_order)


def exchange_kernel(send_ref, colour_ref, opacity_ref, out_ref, landed, send_sem, recv_sem):
    devices = send_ref.shape[0]
    rows = send_ref.shape[1]
    members = lax.axis_size("tile")
    me = lax.axis_index("grp") * members + lax.axis_index("tile")

    def copy_to(dest, source):
        return pltpu.make_async_remote_copy(
            src_ref=send_ref.at[pl.ds(dest, 1)],
            dst_ref=landed.at[pl.ds(source, 1)],
            send_sem=send_sem,
            recv_sem=recv_sem.at[source],
            device_id=(dest // members, dest % members),
            device_id_type=pl.DeviceIdType.MESH,
        )

    def send(k, carry):
        copy_to(lax.rem(me + k, devices), me).start()
        return carry

    lax.fori_loop(1, devices, send, 0)
    landed[pl.ds(me, 1)] = send_ref[pl.ds(me, 1)]
    sample = make_sampler(colour_ref, opacity_ref, 2 * rows)
    tiles = devices // 2
    first = me // 2

    def shade(i, carry):
        m = lax.rem(first - i + tiles, tiles)
        for e in range(2):
            source = 2 * m + e

            @pl.when(source != me)
            def _():
                copy_to(me, source).wait_recv()

        v = jnp.concatenate([landed[2 * m], landed[2 * m + 1]], axis=0)
        part = shade_tile(sample, v)
        for c in range(len(part)):
            out_ref[c, m] = part[c]
        return carry

    lax.fori_loop(0, tiles, shade, 0)
    everything = pltpu.make_async_remote_copy(
        src_ref=send_ref.at[pl.ds(0, devices - 1)],
        dst_ref=landed.at[pl.ds(0, devices - 1)],
        send_sem=send_sem,
        recv_sem=recv_sem.at[me],
        device_id=(me // members, me % members),
        device_id_type=pl.DeviceIdType.MESH,
    )
    everything.wait_send()


def exchange_and_shade(rows, colour_table, opacity_table):
    devices, sub, lanes = rows.shape
    channels = colour_table.shape[0] + 1
    vmem = pl.BlockSpec(memory_space=pltpu.VMEM)
    return pl.pallas_call(
        exchange_kernel,
        out_shape=jax.ShapeDtypeStruct((channels, devices // 2, 2 * sub, lanes), jnp.float32),
        in_specs=[vmem, vmem, vmem],
        out_specs=vmem,
        scratch_shapes=[
            pltpu.VMEM(rows.shape, rows.dtype),
            pltpu.SemaphoreType.DMA,
            pltpu.SemaphoreType.DMA((devices,)),
        ],
        compiler_params=pltpu.CompilerParams(has_side_effects=True),
    )(rows, colour_table, opacity_table.reshape(1, -1))


def body(bricks, colour_table, opacity_table, depth_order):
    groups = lax.axis_size("grp")
    members = lax.axis_size("tile")
    devices = groups * members
    depth = bricks.shape[0]
    pixels = bricks.shape[1] * bricks.shape[2]
    block = pixels // devices
    rows = jnp.transpose(bricks.reshape(depth, devices, block), (1, 0, 2))
    rows = rows.reshape(devices, depth * block // LANES, LANES)
    partials = exchange_and_shade(rows, colour_table, opacity_table)
    return composite(partials, depth_order)


def solution(mesh):
    in_specs = (P(("grp", "tile"), None, None), P(), P(), P())
    out_specs = P(None, ("grp", "tile"))
    return jax.shard_map(body, mesh=mesh, in_specs=in_specs, out_specs=out_specs, check_vma=False)
```

time: 51.4 us -> 54.1 us (1.053)
  Pallas kernels: 48.3 us -> 51 us
    pallas_call x2, Pallas kernels: 48.3 us -> 51 us  [the longest x1 46.1 us: exchange_and_shade(): pl.pallas_call(exchange_kernel, out_shape=jax.ShapeDtypeStruct((channels,...]
where the time goes in v6:
time: 54.1 us; the launch traced here: 53.9 us
  Pallas kernels  51 us (94%)
  local copies, waits for them, and re-layouts  2.85 us (5%)
    pallas_call x1, Pallas kernels, exchange_and_shade(): pl.pallas_call(exchange_kernel, out_shape=jax.ShapeDtypeStruct((channels,...  46.1 us
    pallas_call x1, Pallas kernels, composite(): pl.pallas_call(functools.partial(composite_kernel, members), out_shape=ja...  4.98 us
    reshape x2, local copies, waits for them, and re-layouts, body(): rows = jnp.transpose(bricks.reshape(depth, devices, block), (1, 0, 2))  1.54 us
    reshape x1, local copies, waits for them, and re-layouts, body(): rows = rows.reshape(devices, depth * block // LANES, LANES)  1.31 us

profile of v6, /device:TPU:1, one launch (start us, length us, event | category | flops | bytes accessed | tf_op | source)
XLA Modules:
  0.0 53.9 jit_solution(7561402739545565140)
XLA Ops:
  0.0 1.1 %reshape.9 = f32[2,256,256]{2,1,0:T(8,128)S(1)} reshape(f32[2,128,512]{2,1,0:T(8,128)} %param.4) | data formatting | bytes 1048576 | tf_op jit(solution)/shard_map/reshape | solution.py:185
  1.1 0.4 copy.7
  1.5 1.3 %reshape.10.send_ref = f32[256,4,128]{2,1,0:T(4,128)} reshape(f32[256,2,256]{2,1,0:T(2,128)S(1)} %bitcast.4) | data formatting | bytes 1048576 | tf_op jit(solution)/shard_map/reshape | solution.py:186
  2.9 46.1 %shard_map.46.partial_ref = f32[4,128,8,128]{3,2,1,0:T(8,128)} custom-call(f32[256,4,128]{2,1,0:T(4,128)} %reshape.10.send_ref, f32[3,256]{1,0:T(4,128)} %colour_ref.1, f32[1,256]{1,0:T(1,128)} %bitcast.5), custom_call_target="tpu_custom_call" | custom-call | tf_op jit(solution)/shard_map/pallas_call | solution.py:164
  48.9 5.0 %shard_map.47 = f32[4,256]{1,0:T(4,128)} custom-call(f32[4,128,8,128]{3,2,1,0:T(8,128)} %shard_map.46.partial_ref, s32[4,64]{1,0:T(4,128)} %order_ref.1), custom_call_target="tpu_custom_call" | custom-call | tf_op jit(solution)/shard_map/pallas_call | solution.py:98

commit v7 on v4

--- a/solution.py
+++ b/solution.py
@@ -95,54 +95,83 @@
     )(tiles, colour_table, opacity_table.reshape(1, -1), depth_order)
 
 
-def exchange_kernel(send_ref, out_ref, landed, send_sem, recv_sem, own_sem):
-    devices = send_ref.shape[0]
-    members = lax.axis_size("tile")
-    me = lax.axis_index("grp") * members + lax.axis_index("tile")
+def exchange_kernel(send_ref, out_ref, middle, landed, sems):
+    members, groups = send_ref.shape[0], send_ref.shape[1]
+    g = lax.axis_index("grp")
+    t = lax.axis_index("tile")
+    send1, recv1, send2, recv2, own = (sems.at[i] for i in range(5))
 
-    def send(k, carry):
-        dest = lax.rem(me + k, devices)
+    def first(k, carry):
+        peer = lax.rem(t + k, members)
         pltpu.make_async_remote_copy(
-            src_ref=send_ref.at[pl.ds(dest, 1)],
-            dst_ref=landed.at[pl.ds(me, 1)],
-            send_sem=send_sem,
-            recv_sem=recv_sem,
-            device_id=(dest // members, dest % members),
+            src_ref=send_ref.at[pl.ds(peer, 1)],
+            dst_ref=middle.at[pl.ds(t, 1)],
+            send_sem=send1,
+            recv_sem=recv1,
+            device_id=(g, peer),
             device_id_type=pl.DeviceIdType.MESH,
         ).start()
         return carry
 
-    lax.fori_loop(1, devices, send, 0)
-    own = pltpu.make_async_copy(send_ref.at[pl.ds(me, 1)], landed.at[pl.ds(me, 1)], own_sem)
-    own.start()
-    own.wait()
-    everything = pltpu.make_async_remote_copy(
-        src_ref=send_ref.at[pl.ds(0, devices - 1)],
-        dst_ref=landed.at[pl.ds(0, devices - 1)],
-        send_sem=send_sem,
-        recv_sem=recv_sem,
-        device_id=(me // members, me % members),
+    lax.fori_loop(1, members, first, 0)
+    middle[pl.ds(t, 1)] = send_ref[pl.ds(t, 1)]
+    stage1 = pltpu.make_async_remote_copy(
+        src_ref=send_ref.at[pl.ds(0, members - 1)],
+        dst_ref=middle.at[pl.ds(0, members - 1)],
+        send_sem=send1,
+        recv_sem=recv1,
+        device_id=(g, t),
         device_id_type=pl.DeviceIdType.MESH,
     )
-    everything.wait_send()
-    everything.wait_recv()
+    stage1.wait_recv()
+
+    def second(k, carry):
+        peer = lax.rem(g + k, groups)
+        pltpu.make_async_remote_copy(
+            src_ref=middle.at[:, peer],
+            dst_ref=landed.at[g],
+            send_sem=send2,
+            recv_sem=recv2,
+            device_id=(peer, t),
+            device_id_type=pl.DeviceIdType.MESH,
+        ).start()
+        return carry
+
+    lax.fori_loop(1, groups, second, 0)
+    mine = pltpu.make_async_copy(middle.at[:, g], landed.at[g], own)
+    mine.start()
+    mine.wait()
+    stage2 = pltpu.make_async_remote_copy(
+        src_ref=landed.at[pl.ds(0, groups - 1)],
+        dst_ref=landed.at[pl.ds(0, groups - 1)],
+        send_sem=send2,
+        recv_sem=recv2,
+        device_id=(g, t),
+        device_id_type=pl.DeviceIdType.MESH,
+    )
+    stage2.wait_recv()
+    stage1.wait_send()
+    stage2.wait_send()
     out_ref[...] = landed[...]
 
 
-def exchange(rows):
-    return pl.pallas_call(
+def exchange(rows, groups):
+    devices, sub, lanes = rows.shape
+    members = devices // groups
+    send = jnp.transpose(rows.reshape(groups, members, sub, lanes), (1, 0, 2, 3))
+    arrived = pl.pallas_call(
         exchange_kernel,
-        out_shape=jax.ShapeDtypeStruct(rows.shape, rows.dtype),
+        out_shape=jax.ShapeDtypeStruct((groups, members, sub, lanes), rows.dtype),
         in_specs=[pl.BlockSpec(memory_space=pltpu.VMEM)],
         out_specs=pl.BlockSpec(memory_space=pltpu.VMEM),
         scratch_shapes=[
-            pltpu.VMEM(rows.shape, rows.dtype),
-            pltpu.SemaphoreType.DMA,
-            pltpu.SemaphoreType.DMA,
-            pltpu.SemaphoreType.DMA,
+            pltpu.VMEM((members, groups, sub, lanes), rows.dtype),
+            pltpu.VMEM((groups, members, sub, lanes), rows.dtype),
+            pltpu.SemaphoreType.DMA((5,)),
         ],
         compiler_params=pltpu.CompilerParams(has_side_effects=True),
-    )(rows)
+    )(send)
+    return arrived.reshape(devices, sub, lanes)
 
 
 def body(bricks, colour_table, opacity_table, depth_order):
@@ -154,7 +183,7 @@
     block = pixels // devices
     rows = jnp.transpose(bricks.reshape(depth, devices, block), (1, 0, 2))
     rows = rows.reshape(devices, depth * block // LANES, LANES)
-    arrived = exchange(rows)
+    arrived = exchange(rows, groups)
     return render(arrived, colour_table, opacity_table, depth_order)
 
 

time: 51.4 us -> 58.1 us (1.13); the launches traced: 51.2 us -> 57.1 us
  Pallas kernels: 48.3 us -> 54.2 us
    pallas_call x1, Pallas kernels: 36.7 us -> 42.6 us  [exchange(): pl.pallas_call(exchange_kernel, out_shape=jax.ShapeDtypeStruct((groups, m...]
    another operation x0 -> x2, local copies, waits for them, and re-layouts: none -> 1.39 us  [exchange(): rows.reshape(groups, members, sub, lanes)]
    reshape x1 -> x0, local copies, waits for them, and re-layouts: 1.3 us -> none  [body(): rows = rows.reshape(devices, depth * block // LANES, LANES)]
where the time goes in v7:
time: 58.1 us; the launch traced here: 57.1 us
  Pallas kernels  54.2 us (93%)
  local copies, waits for them, and re-layouts  2.93 us (5%)
    pallas_call x1, Pallas kernels, exchange(): pl.pallas_call(exchange_kernel, out_shape=jax.ShapeDtypeStruct((groups, m...  42.6 us
    pallas_call x1, Pallas kernels, render(): pl.pallas_call(functools.partial(render_kernel, members), out_shape=jax.S...  11.6 us
    reshape x2, local copies, waits for them, and re-layouts, body(): rows = jnp.transpose(bricks.reshape(depth, devices, block), (1, 0, 2))  1.54 us
    another operation x2, local copies, waits for them, and re-layouts, exchange(): rows.reshape(groups, members, sub, lanes)  1.39 us

profile of v7, /device:TPU:1, one launch (start us, length us, event | category | flops | bytes accessed | tf_op | source)
XLA Modules:
  0.0 57.1 jit_solution(13072131943613278415)
XLA Ops:
  0.0 1.1 %reshape.6 = f32[2,256,256]{2,1,0:T(8,128)S(1)} reshape(f32[2,128,512]{2,1,0:T(8,128)} %param.4) | data formatting | bytes 1048576 | tf_op jit(solution)/shard_map/reshape | solution.py:184
  1.1 0.4 copy.10
  1.5 0.5 reshape_reshape.6
  2.1 0.9 %copy.9 = f32[4,64,4,128]{3,2,0,1:T(4,128)} copy(f32[4,64,4,128]{3,2,1,0:T(4,128)S(1)} %reshape_reshape.6) | data formatting | bytes 1048576 | tf_op jit(solution)/shard_map/reshape;reshape | solution.py:161
  2.9 42.6 %shard_map.46 = f32[4,64,4,128]{3,2,1,0:T(4,128)} custom-call(f32[64,4,4,128]{3,2,1,0:T(4,128)} %bitcast.9), custom_call_target="tpu_custom_call" | custom-call | tf_op jit(solution)/shard_map/pallas_call | solution.py:162
  45.5 11.6 %shard_map.47 = f32[4,256]{1,0:T(4,128)} custom-call(f32[128,8,128]{2,1,0:T(8,128)} %bitcast.10, f32[3,256]{1,0:T(4,128)} %colour_ref.1, f32[1,256]{1,0:T(1,128)} %bitcast.11, s32[4,64]{1,0:T(4,128)} %order_ref.1), custom_call_target="tpu_custom_call" | custom-call | tf_op jit(solution)/shard_map/pallas_call | solution.py:89

commit v8 on v4

--- a/solution.py
+++ b/solution.py
@@ -21,14 +21,19 @@
         [jnp.broadcast_to(r[:, h * lanes : (h + 1) * lanes], (sub, lanes)) for h in range(halves)]
         for r in rows
     ]
+    last_lane = lax.broadcasted_iota(jnp.int32, (sub, lanes), 1) == lanes - 1
+    uppers = []
+    for per_half in tables:
+        shifted = [pltpu.roll(x, lanes - 1, 1) for x in per_half]
+        uppers.append(
+            [jnp.where(last_lane, shifted[h + 1], shifted[h]) if h + 1 < halves else shifted[h] for h in range(halves)]
+        )
 
-    def pick(c, index):
-        lane = index % lanes
-        half = index // lanes
-        got = jnp.take_along_axis(tables[c][0], lane, axis=1, mode="promise_in_bounds")
+    def pick(table, lane, in_half):
+        got = jnp.take_along_axis(table[0], lane, axis=1, mode="promise_in_bounds")
         for h in range(1, halves):
-            other = jnp.take_along_axis(tables[c][h], lane, axis=1, mode="promise_in_bounds")
-            got = jnp.where(half == h, other, got)
+            other = jnp.take_along_axis(table[h], lane, axis=1, mode="promise_in_bounds")
+            got = jnp.where(in_half[h], other, got)
         return got
 
     def sample(v):
@@ -36,7 +41,13 @@
         lower = jnp.clip(jnp.floor(u), 0.0, float(knots - 2))
         frac = u - lower
         index = lower.astype(jnp.int32)
-        return [pick(c, index) * (1.0 - frac) + pick(c, index + 1) * frac for c in range(colours + 1)]
+        lane = index % lanes
+        half = index // lanes
+        in_half = [None] + [half == h for h in range(1, halves)]
+        return [
+            pick(tables[c], lane, in_half) * (1.0 - frac) + pick(uppers[c], lane, in_half) * frac
+            for c in range(colours + 1)
+        ]
 
     def shade(m, carry):
         front = sample(values_ref[m])
@@ -56,7 +67,7 @@
                 parts_ref[c, place] = part[c] if e == 0 else pltpu.roll(part[c], sub - 4, 0)
         return carry
 
-    lax.fori_loop(0, tiles, shade, 0, unroll=2)
+    lax.fori_loop(0, tiles, shade, 0, unroll=4)
 
     def blend(k, pics):
         out = []

time: 51.4 us -> 47.2 us (0.918)
  Pallas kernels: 48.3 us -> 44.2 us
    pallas_call x1, Pallas kernels: 11.6 us -> 7.45 us  [render(): pl.pallas_call(functools.partial(render_kernel, members), out_shape=jax.S...]
where the time goes in v8:
time: 47.2 us; the launch traced here: 47.1 us
  Pallas kernels  44.2 us (94%)
  local copies, waits for them, and re-layouts  2.84 us (6%)
    pallas_call x1, Pallas kernels, exchange(): pl.pallas_call(exchange_kernel, out_shape=jax.ShapeDtypeStruct(rows.shape...  36.7 us
    pallas_call x1, Pallas kernels, render(): pl.pallas_call(functools.partial(render_kernel, members), out_shape=jax.S...  7.45 us
    reshape x2, local copies, waits for them, and re-layouts, body(): rows = jnp.transpose(bricks.reshape(depth, devices, block), (1, 0, 2))  1.54 us
    reshape x1, local copies, waits for them, and re-layouts, body(): rows = rows.reshape(devices, depth * block // LANES, LANES)  1.3 us

profile of v8, /device:TPU:1, one launch (start us, length us, event | category | flops | bytes accessed | tf_op | source)
XLA Modules:
  0.0 47.1 jit_solution(3129160062842811233)
XLA Ops:
  0.0 1.1 %reshape.12 = f32[2,256,256]{2,1,0:T(8,128)S(1)} reshape(f32[2,128,512]{2,1,0:T(8,128)} %param.4) | data formatting | bytes 1048576 | tf_op jit(solution)/shard_map/reshape | solution.py:166
  1.1 0.4 copy.7
  1.5 1.3 %reshape.13.send_ref = f32[256,4,128]{2,1,0:T(4,128)} reshape(f32[256,2,256]{2,1,0:T(2,128)S(1)} %bitcast.5) | data formatting | bytes 1048576 | tf_op jit(solution)/shard_map/reshape | solution.py:167
  2.8 36.7 %shard_map.46 = f32[256,4,128]{2,1,0:T(4,128)} custom-call(f32[256,4,128]{2,1,0:T(4,128)} %reshape.13.send_ref), custom_call_target="tpu_custom_call" | custom-call | tf_op jit(solution)/shard_map/pallas_call | solution.py:144
  39.6 7.5 %shard_map.47 = f32[4,256]{1,0:T(4,128)} custom-call(f32[128,8,128]{2,1,0:T(8,128)} %bitcast.6, f32[3,256]{1,0:T(4,128)} %colour_ref.1, f32[1,256]{1,0:T(1,128)} %bitcast.7, s32[4,64]{1,0:T(4,128)} %order_ref.1), custom_call_target="tpu_custom_call" | custom-call | tf_op jit(solution)/shard_map/pallas_call | solution.py:100

commit v9 on v8

--- a/solution.py
+++ b/solution.py
@@ -67,7 +67,7 @@
                 parts_ref[c, place] = part[c] if e == 0 else pltpu.roll(part[c], sub - 4, 0)
         return carry
 
-    lax.fori_loop(0, tiles, shade, 0, unroll=4)
+    lax.fori_loop(0, tiles, shade, 0, unroll=16)
 
     def blend(k, pics):
         out = []

time: 47.2 us -> 45.2 us (0.958)
  Pallas kernels: 44.2 us -> 42.2 us
    pallas_call x1, Pallas kernels: 7.45 us -> 5.44 us  [render(): pl.pallas_call(functools.partial(render_kernel, members), out_shape=jax.S...]
where the time goes in v9:
time: 45.2 us; the launch traced here: 45 us
  Pallas kernels  42.2 us (93%)
  local copies, waits for them, and re-layouts  2.84 us (6%)
    pallas_call x1, Pallas kernels, exchange(): pl.pallas_call(exchange_kernel, out_shape=jax.ShapeDtypeStruct(rows.shape...  36.7 us
    pallas_call x1, Pallas kernels, render(): pl.pallas_call(functools.partial(render_kernel, members), out_shape=jax.S...  5.44 us
    reshape x2, local copies, waits for them, and re-layouts, body(): rows = jnp.transpose(bricks.reshape(depth, devices, block), (1, 0, 2))  1.54 us
    reshape x1, local copies, waits for them, and re-layouts, body(): rows = rows.reshape(devices, depth * block // LANES, LANES)  1.3 us

profile of v9, /device:TPU:1, one launch (start us, length us, event | category | flops | bytes accessed | tf_op | source)
XLA Modules:
  0.0 45.0 jit_solution(16445241287795117998)
XLA Ops:
  0.0 1.1 %reshape.12 = f32[2,256,256]{2,1,0:T(8,128)S(1)} reshape(f32[2,128,512]{2,1,0:T(8,128)} %param.4) | data formatting | bytes 1048576 | tf_op jit(solution)/shard_map/reshape | solution.py:166
  1.1 0.4 copy.7
  1.5 1.3 %reshape.13.send_ref = f32[256,4,128]{2,1,0:T(4,128)} reshape(f32[256,2,256]{2,1,0:T(2,128)S(1)} %bitcast.5) | data formatting | bytes 1048576 | tf_op jit(solution)/shard_map/reshape | solution.py:167
  2.8 36.7 %shard_map.46 = f32[256,4,128]{2,1,0:T(4,128)} custom-call(f32[256,4,128]{2,1,0:T(4,128)} %reshape.13.send_ref), custom_call_target="tpu_custom_call" | custom-call | tf_op jit(solution)/shard_map/pallas_call | solution.py:144
  39.6 5.4 %shard_map.47 = f32[4,256]{1,0:T(4,128)} custom-call(f32[128,8,128]{2,1,0:T(8,128)} %bitcast.6, f32[3,256]{1,0:T(4,128)} %colour_ref.1, f32[1,256]{1,0:T(1,128)} %bitcast.7, s32[4,64]{1,0:T(4,128)} %order_ref.1), custom_call_target="tpu_custom_call" | custom-call | tf_op jit(solution)/shard_map/pallas_call | solution.py:100

commit v10 on v9

--- a/solution.py
+++ b/solution.py
@@ -106,16 +106,41 @@
     )(tiles, colour_table, opacity_table.reshape(1, -1), depth_order)
 
 
+def arrange_kernel(block, bricks_ref, out_ref):
+    depth, height, width = bricks_ref.shape
+    per_row = width // block
+    parts = block // LANES
+    chunk = depth * parts
+    for s in range(depth):
+        for col in range(width // LANES):
+            h, j = divmod(col, parts)
+            for r in range(0, height, 8):
+                start = (per_row * r + h) * chunk + s * parts + j
+                out_ref[pl.ds(start, 8, stride=per_row * chunk), :] = bricks_ref[s, pl.ds(r, 8), pl.ds(col * LANES, LANES)]
+
+
+def arrange(bricks, devices):
+    depth, height, width = bricks.shape
+    block = height * width // devices
+    vmem = pl.BlockSpec(memory_space=pltpu.VMEM)
+    return pl.pallas_call(
+        functools.partial(arrange_kernel, block),
+        out_shape=jax.ShapeDtypeStruct((height * width * depth // LANES, LANES), bricks.dtype),
+        in_specs=[vmem],
+        out_specs=vmem,
+    )(bricks)
+
+
 def exchange_kernel(send_ref, out_ref, landed, send_sem, recv_sem, own_sem):
-    devices = send_ref.shape[0]
+    devices, chunk, lanes = landed.shape
     members = lax.axis_size("tile")
     me = lax.axis_index("grp") * members + lax.axis_index("tile")
 
     def send(k, carry):
         dest = lax.rem(me + k, devices)
         pltpu.make_async_remote_copy(
-            src_ref=send_ref.at[pl.ds(dest, 1)],
-            dst_ref=landed.at[pl.ds(me, 1)],
+            src_ref=send_ref.at[pl.ds(dest * chunk, chunk)],
+            dst_ref=landed.at[me],
             send_sem=send_sem,
             recv_sem=recv_sem,
             device_id=(dest // members, dest % members),
@@ -124,11 +149,11 @@
         return carry
 
     lax.fori_loop(1, devices, send, 0)
-    own = pltpu.make_async_copy(send_ref.at[pl.ds(me, 1)], landed.at[pl.ds(me, 1)], own_sem)
+    own = pltpu.make_async_copy(send_ref.at[pl.ds(me * chunk, chunk)], landed.at[me], own_sem)
     own.start()
     own.wait()
     everything = pltpu.make_async_remote_copy(
-        src_ref=send_ref.at[pl.ds(0, devices - 1)],
+        src_ref=landed.at[pl.ds(0, devices - 1)],
         dst_ref=landed.at[pl.ds(0, devices - 1)],
         send_sem=send_sem,
         recv_sem=recv_sem,
@@ -140,32 +165,30 @@
     out_ref[...] = landed[...]
 
 
-def exchange(rows):
+def exchange(flat, devices):
+    chunk = flat.shape[0] // devices
+    shape = (devices, chunk, flat.shape[1])
     return pl.pallas_call(
         exchange_kernel,
-        out_shape=jax.ShapeDtypeStruct(rows.shape, rows.dtype),
+        out_shape=jax.ShapeDtypeStruct(shape, flat.dtype),
         in_specs=[pl.BlockSpec(memory_space=pltpu.VMEM)],
         out_specs=pl.BlockSpec(memory_space=pltpu.VMEM),
         scratch_shapes=[
-            pltpu.VMEM(rows.shape, rows.dtype),
+            pltpu.VMEM(shape, flat.dtype),
             pltpu.SemaphoreType.DMA,
             pltpu.SemaphoreType.DMA,
             pltpu.SemaphoreType.DMA,
         ],
         compiler_params=pltpu.CompilerParams(has_side_effects=True),
-    )(rows)
+    )(flat)
 
 
 def body(bricks, colour_table, opacity_table, depth_order):
     groups = lax.axis_size("grp")
     members = lax.axis_size("tile")
     devices = groups * members
-    depth = bricks.shape[0]
-    pixels = bricks.shape[1] * bricks.shape[2]
-    block = pixels // devices
-    rows = jnp.transpose(bricks.reshape(depth, devices, block), (1, 0, 2))
-    rows = rows.reshape(devices, depth * block // LANES, LANES)
-    arrived = exchange(rows)
+    flat = arrange(bricks, devices)
+    arrived = exchange(flat, devices)
     return render(arrived, colour_table, opacity_table, depth_order)
 
 

time: 45.2 us -> 44.3 us (0.980)
  local copies, waits for them, and re-layouts: 2.84 us -> 0 us
  Pallas kernels: 42.2 us -> 44.1 us
    reshape x3 -> x0, local copies, waits for them, and re-layouts: 2.84 us -> none  [the longest x2 1.54 us: body(): rows = jnp.transpose(bricks.reshape(depth, devices, block), (1, 0, 2))]
    pallas_call x1 -> x2, Pallas kernels: 36.7 us -> 38.7 us  [the longest x1 36.7 us: exchange(): pl.pallas_call(exchange_kernel, out_shape=jax.ShapeDtypeStruct(shape, fla...]
where the time goes in v10:
time: 44.3 us; the launch traced here: 44.1 us
  Pallas kernels  44.1 us (100%)
    pallas_call x1, Pallas kernels, exchange(): pl.pallas_call(exchange_kernel, out_shape=jax.ShapeDtypeStruct(shape, fla...  36.7 us
    pallas_call x1, Pallas kernels, render(): pl.pallas_call(functools.partial(render_kernel, members), out_shape=jax.S...  5.44 us
    pallas_call x1, Pallas kernels, arrange(): pl.pallas_call(functools.partial(arrange_kernel, block), out_shape=jax.Sh...  1.95 us

profile of v10, /device:TPU:1, one launch (start us, length us, event | category | flops | bytes accessed | tf_op | source)
XLA Modules:
  0.0 44.1 jit_solution(9128487967048598002)
XLA Ops:
  0.0 2.0 %shard_map.46.send_ref = f32[1024,128]{1,0:T(8,128)} custom-call(f32[2,128,512]{2,1,0:T(8,128)} %bricks_ref.1), custom_call_target="tpu_custom_call" | custom-call | tf_op jit(solution)/shard_map/pallas_call | solution.py:126
  2.0 36.7 %shard_map.47 = f32[256,4,128]{2,1,0:T(4,128)} custom-call(f32[1024,128]{1,0:T(8,128)} %shard_map.46.send_ref), custom_call_target="tpu_custom_call" | custom-call | tf_op jit(solution)/shard_map/pallas_call | solution.py:171
  38.7 5.4 %shard_map.48 = f32[4,256]{1,0:T(4,128)} custom-call(f32[128,8,128]{2,1,0:T(8,128)} %bitcast.2, f32[3,256]{1,0:T(4,128)} %colour_ref.1, f32[1,256]{1,0:T(1,128)} %bitcast.3, s32[4,64]{1,0:T(4,128)} %order_ref.1), custom_call_target="tpu_custom_call" | custom-call | tf_op jit(solution)/shard_map/pallas_call | solution.py:100

commit v11 on v10

--- a/solution.py
+++ b/solution.py
@@ -67,7 +67,7 @@
                 parts_ref[c, place] = part[c] if e == 0 else pltpu.roll(part[c], sub - 4, 0)
         return carry
 
-    lax.fori_loop(0, tiles, shade, 0, unroll=16)
+    lax.fori_loop(0, tiles, shade, 0, unroll=32)
 
     def blend(k, pics):
         out = []
@@ -79,7 +79,7 @@
 
     zero = jnp.zeros((sub, lanes), jnp.float32)
     start = tuple(tuple(zero for _ in range(colours + 1)) for _ in range(groups))
-    pics = lax.fori_loop(0, members, blend, start, unroll=4)
+    pics = lax.fori_loop(0, members, blend, start, unroll=8)
     final = pics[0]
     for g in range(1, groups):
         clear = 1.0 - final[colours]

time: 44.3 us -> 43.9 us (level)
  no operation moved by 1% of the time
where the time goes in v11:
time: 43.9 us; the launch traced here: 43.7 us
  Pallas kernels  43.7 us (100%)
    pallas_call x1, Pallas kernels, exchange(): pl.pallas_call(exchange_kernel, out_shape=jax.ShapeDtypeStruct(shape, fla...  36.7 us
    pallas_call x1, Pallas kernels, render(): pl.pallas_call(functools.partial(render_kernel, members), out_shape=jax.S...  5.01 us
    pallas_call x1, Pallas kernels, arrange(): pl.pallas_call(functools.partial(arrange_kernel, block), out_shape=jax.Sh...  1.95 us

profile of v11, /device:TPU:1, one launch (start us, length us, event | category | flops | bytes accessed | tf_op | source)
XLA Modules:
  0.0 43.7 jit_solution(4428501892624098172)
XLA Ops:
  0.0 2.0 %shard_map.46.send_ref = f32[1024,128]{1,0:T(8,128)} custom-call(f32[2,128,512]{2,1,0:T(8,128)} %bricks_ref.1), custom_call_target="tpu_custom_call" | custom-call | tf_op jit(solution)/shard_map/pallas_call | solution.py:126
  2.0 36.7 %shard_map.47 = f32[256,4,128]{2,1,0:T(4,128)} custom-call(f32[1024,128]{1,0:T(8,128)} %shard_map.46.send_ref), custom_call_target="tpu_custom_call" | custom-call | tf_op jit(solution)/shard_map/pallas_call | solution.py:171
  38.7 5.0 %shard_map.48 = f32[4,256]{1,0:T(4,128)} custom-call(f32[128,8,128]{2,1,0:T(8,128)} %bitcast.2, f32[3,256]{1,0:T(4,128)} %colour_ref.1, f32[1,256]{1,0:T(1,128)} %bitcast.3, s32[4,64]{1,0:T(4,128)} %order_ref.1), custom_call_target="tpu_custom_call" | custom-call | tf_op jit(solution)/shard_map/pallas_call | solution.py:100

commit v12 on v11

--- a/solution.py
+++ b/solution.py
@@ -136,14 +136,20 @@
     members = lax.axis_size("tile")
     me = lax.axis_index("grp") * members + lax.axis_index("tile")
 
+    groups = devices // members
+    g = lax.axis_index("grp")
+    t = lax.axis_index("tile")
+
     def send(k, carry):
-        dest = lax.rem(me + k, devices)
+        peer_g = lax.rem(g + k % groups, groups)
+        peer_t = lax.rem(t + k // groups, members)
+        dest = peer_g * members + peer_t
         pltpu.make_async_remote_copy(
             src_ref=send_ref.at[pl.ds(dest * chunk, chunk)],
             dst_ref=landed.at[me],
             send_sem=send_sem,
             recv_sem=recv_sem,
-            device_id=(dest // members, dest % members),
+            device_id=(peer_g, peer_t),
             device_id_type=pl.DeviceIdType.MESH,
         ).start()
         return carry

time: 43.9 us -> 43.7 us (level); the launches traced: 43.7 us -> 43 us
  Pallas kernels: 43.7 us -> 43 us
    pallas_call x1, Pallas kernels: 36.7 us -> 36 us  [exchange(): pl.pallas_call(exchange_kernel, out_shape=jax.ShapeDtypeStruct(shape, fla...]
where the time goes in v12:
time: 43.7 us; the launch traced here: 43 us
  Pallas kernels  43 us (98%)
    pallas_call x1, Pallas kernels, exchange(): pl.pallas_call(exchange_kernel, out_shape=jax.ShapeDtypeStruct(shape, fla...  36 us
    pallas_call x1, Pallas kernels, render(): pl.pallas_call(functools.partial(render_kernel, members), out_shape=jax.S...  5.02 us
    pallas_call x1, Pallas kernels, arrange(): pl.pallas_call(functools.partial(arrange_kernel, block), out_shape=jax.Sh...  1.95 us

profile of v12, /device:TPU:1, one launch (start us, length us, event | category | flops | bytes accessed | tf_op | source)
XLA Modules:
  0.0 43.0 jit_solution(15247743556347977899)
XLA Ops:
  0.0 2.0 %shard_map.46.send_ref = f32[1024,128]{1,0:T(8,128)} custom-call(f32[2,128,512]{2,1,0:T(8,128)} %bricks_ref.1), custom_call_target="tpu_custom_call" | custom-call | tf_op jit(solution)/shard_map/pallas_call | solution.py:126
  2.0 36.0 %shard_map.47 = f32[256,4,128]{2,1,0:T(4,128)} custom-call(f32[1024,128]{1,0:T(8,128)} %shard_map.46.send_ref), custom_call_target="tpu_custom_call" | custom-call | tf_op jit(solution)/shard_map/pallas_call | solution.py:177
  38.0 5.0 %shard_map.48 = f32[4,256]{1,0:T(4,128)} custom-call(f32[128,8,128]{2,1,0:T(8,128)} %bitcast.2, f32[3,256]{1,0:T(4,128)} %colour_ref.1, f32[1,256]{1,0:T(1,128)} %bitcast.3, s32[4,64]{1,0:T(4,128)} %order_ref.1), custom_call_target="tpu_custom_call" | custom-call | tf_op jit(solution)/shard_map/pallas_call | solution.py:100

commit v13 on v12

--- a/solution.py
+++ b/solution.py
@@ -90,11 +90,10 @@
 
 
 def render(arrived, colour_table, opacity_table, depth_order):
-    devices = arrived.shape[0]
+    pairs, sub, lanes = arrived.shape
+    devices = 2 * pairs
     groups, members = depth_order.shape
-    lanes = arrived.shape[2]
-    sub = 2 * arrived.shape[1]
-    tiles = arrived.reshape(devices // 2, sub, lanes)
+    tiles = arrived
     channels = colour_table.shape[0] + 1
     vmem = pl.BlockSpec(memory_space=pltpu.VMEM)
     return pl.pallas_call(
@@ -131,49 +130,67 @@
     )(bricks)
 
 
-def exchange_kernel(send_ref, out_ref, landed, send_sem, recv_sem, own_sem):
-    devices, chunk, lanes = landed.shape
+def exchange_kernel(send_ref, out_ref, middle, landed, sems):
+    pairs, sub, lanes = send_ref.shape
+    half = sub // 2
     members = lax.axis_size("tile")
-    me = lax.axis_index("grp") * members + lax.axis_index("tile")
-
-    groups = devices // members
+    pair_members = members // 2
+    groups = pairs // pair_members
     g = lax.axis_index("grp")
     t = lax.axis_index("tile")
+    core = t % 2
+    mine = (g * members + t) // 2
+    send1, recv1, send2, recv2, own1, own2 = (sems.at[i] for i in range(6))
+    partner = pltpu.make_async_remote_copy(
+        src_ref=send_ref.at[:, pl.ds((1 - core) * half, half), :],
+        dst_ref=middle.at[:, pl.ds(core * half, half), :],
+        send_sem=send1,
+        recv_sem=recv1,
+        device_id=(g, t + 1 - 2 * core),
+        device_id_type=pl.DeviceIdType.MESH,
+    )
+    partner.start()
+    kept = pltpu.make_async_copy(
+        send_ref.at[:, pl.ds(core * half, half), :], middle.at[:, pl.ds(core * half, half), :], own1
+    )
+    kept.start()
+    kept.wait()
+    partner.wait_recv()
 
     def send(k, carry):
         peer_g = lax.rem(g + k % groups, groups)
-        peer_t = lax.rem(t + k // groups, members)
-        dest = peer_g * members + peer_t
+        peer_p = lax.rem(t // 2 + k // groups, pair_members)
         pltpu.make_async_remote_copy(
-            src_ref=send_ref.at[pl.ds(dest * chunk, chunk)],
-            dst_ref=landed.at[me],
-            send_sem=send_sem,
-            recv_sem=recv_sem,
-            device_id=(peer_g, peer_t),
+            src_ref=middle.at[peer_g * pair_members + peer_p],
+            dst_ref=landed.at[mine],
+            send_sem=send2,
+            recv_sem=recv2,
+            device_id=(peer_g, 2 * peer_p + core),
             device_id_type=pl.DeviceIdType.MESH,
         ).start()
         return carry
 
-    lax.fori_loop(1, devices, send, 0)
-    own = pltpu.make_async_copy(send_ref.at[pl.ds(me * chunk, chunk)], landed.at[me], own_sem)
-    own.start()
-    own.wait()
+    lax.fori_loop(1, pairs, send, 0)
+    local = pltpu.make_async_copy(middle.at[mine], landed.at[mine], own2)
+    local.start()
+    local.wait()
     everything = pltpu.make_async_remote_copy(
-        src_ref=landed.at[pl.ds(0, devices - 1)],
-        dst_ref=landed.at[pl.ds(0, devices - 1)],
-        send_sem=send_sem,
-        recv_sem=recv_sem,
-        device_id=(me // members, me % members),
+        src_ref=landed.at[pl.ds(0, pairs - 1)],
+        dst_ref=landed.at[pl.ds(0, pairs - 1)],
+        send_sem=send2,
+        recv_sem=recv2,
+        device_id=(g, t),
         device_id_type=pl.DeviceIdType.MESH,
     )
+    everything.wait_recv()
+    partner.wait_send()
     everything.wait_send()
-    everything.wait_recv()
     out_ref[...] = landed[...]
 
 
 def exchange(flat, devices):
-    chunk = flat.shape[0] // devices
-    shape = (devices, chunk, flat.shape[1])
+    sub = 2 * flat.shape[0] // devices
+    shape = (devices // 2, sub, flat.shape[1])
     return pl.pallas_call(
         exchange_kernel,
         out_shape=jax.ShapeDtypeStruct(shape, flat.dtype),
@@ -181,12 +198,11 @@
         out_specs=pl.BlockSpec(memory_space=pltpu.VMEM),
         scratch_shapes=[
             pltpu.VMEM(shape, flat.dtype),
-            pltpu.SemaphoreType.DMA,
-            pltpu.SemaphoreType.DMA,
-            pltpu.SemaphoreType.DMA,
+            pltpu.VMEM(shape, flat.dtype),
+            pltpu.SemaphoreType.DMA((6,)),
         ],
         compiler_params=pltpu.CompilerParams(has_side_effects=True),
-    )(flat)
+    )(flat.reshape(shape))
 
 
 def body(bricks, colour_table, opacity_table, depth_order):

time: 43.7 us -> 44.9 us (1.027)
  the two profiles are of different devices: /device:TPU:1 before, /device:TPU:24 now
where the time goes in v13:
time: 44.9 us; the launch traced here: 44.7 us
  Pallas kernels  44.7 us (100%)
    pallas_call x1, Pallas kernels, exchange(): pl.pallas_call(exchange_kernel, out_shape=jax.ShapeDtypeStruct(shape, fla...  37.7 us
    pallas_call x1, Pallas kernels, render(): pl.pallas_call(functools.partial(render_kernel, members), out_shape=jax.S...  5.01 us
    pallas_call x1, Pallas kernels, arrange(): pl.pallas_call(functools.partial(arrange_kernel, block), out_shape=jax.Sh...  1.95 us

profile of v13, /device:TPU:24, one launch (start us, length us, event | category | flops | bytes accessed | tf_op | source)
XLA Modules:
  0.0 44.7 jit_solution(13491714891044189399)
XLA Ops:
  0.0 2.0 %shard_map.46 = f32[1024,128]{1,0:T(8,128)} custom-call(f32[2,128,512]{2,1,0:T(8,128)} %bricks_ref.1), custom_call_target="tpu_custom_call" | custom-call | tf_op jit(solution)/shard_map/pallas_call | solution.py:125
  2.0 37.7 %shard_map.47.values_ref = f32[128,8,128]{2,1,0:T(8,128)} custom-call(f32[128,8,128]{2,1,0:T(8,128)} %bitcast.2), custom_call_target="tpu_custom_call" | custom-call | tf_op jit(solution)/shard_map/pallas_call | solution.py:194
  39.7 5.0 %shard_map.48 = f32[4,256]{1,0:T(4,128)} custom-call(f32[128,8,128]{2,1,0:T(8,128)} %shard_map.47.values_ref, f32[3,256]{1,0:T(4,128)} %colour_ref.1, f32[1,256]{1,0:T(1,128)} %bitcast.3, s32[4,64]{1,0:T(4,128)} %order_ref.1), custom_call_target="tpu_custom_call" | custom-call | tf_op jit(solution)/shard_map/pallas_call | solution.py:99

commit v14 on v12

--- a/solution.py
+++ b/solution.py
@@ -140,9 +140,20 @@
     g = lax.axis_index("grp")
     t = lax.axis_index("tile")
 
+    def peer(k):
+        return lax.rem(g + k % groups, groups), lax.rem(t + k // groups, members)
+
+    barrier = pltpu.get_barrier_semaphore()
+
+    def greet(k, carry):
+        pl.semaphore_signal(barrier, 1, device_id=peer(k), device_id_type=pl.DeviceIdType.MESH)
+        return carry
+
+    lax.fori_loop(1, devices, greet, 0)
+    pl.semaphore_wait(barrier, devices - 1)
+
     def send(k, carry):
-        peer_g = lax.rem(g + k % groups, groups)
-        peer_t = lax.rem(t + k // groups, members)
+        peer_g, peer_t = peer(k)
         dest = peer_g * members + peer_t
         pltpu.make_async_remote_copy(
             src_ref=send_ref.at[pl.ds(dest * chunk, chunk)],
@@ -185,7 +196,7 @@
             pltpu.SemaphoreType.DMA,
             pltpu.SemaphoreType.DMA,
         ],
-        compiler_params=pltpu.CompilerParams(has_side_effects=True),
+        compiler_params=pltpu.CompilerParams(collective_id=0, has_side_effects=True),
     )(flat)
 
 

time: 43.7 us -> 40.6 us (0.929); the launches traced: 43 us -> 40.4 us
  Pallas kernels: 43 us -> 40.4 us
    pallas_call x1, Pallas kernels: 36 us -> 33.5 us  [exchange(): pl.pallas_call(exchange_kernel, out_shape=jax.ShapeDtypeStruct(shape, fla...]
where the time goes in v14:
time: 40.6 us; the launch traced here: 40.4 us
  Pallas kernels  40.4 us (100%)
    pallas_call x1, Pallas kernels, exchange(): pl.pallas_call(exchange_kernel, out_shape=jax.ShapeDtypeStruct(shape, fla...  33.5 us
    pallas_call x1, Pallas kernels, render(): pl.pallas_call(functools.partial(render_kernel, members), out_shape=jax.S...  5.01 us
    pallas_call x1, Pallas kernels, arrange(): pl.pallas_call(functools.partial(arrange_kernel, block), out_shape=jax.Sh...  1.95 us

profile of v14, /device:TPU:1, one launch (start us, length us, event | category | flops | bytes accessed | tf_op | source)
XLA Modules:
  0.0 40.4 jit_solution(15196560399709078587)
XLA Ops:
  0.0 2.0 %shard_map.46.send_ref = f32[1024,128]{1,0:T(8,128)} custom-call(f32[2,128,512]{2,1,0:T(8,128)} %bricks_ref.1), custom_call_target="tpu_custom_call" | custom-call | tf_op jit(solution)/shard_map/pallas_call | solution.py:126
  2.0 33.5 %shard_map.47 = f32[256,4,128]{2,1,0:T(4,128)} custom-call(f32[1024,128]{1,0:T(8,128)} %shard_map.46.send_ref), custom_call_target="tpu_custom_call" | custom-call | tf_op jit(solution)/shard_map/pallas_call | solution.py:188
  35.4 5.0 %shard_map.48 = f32[4,256]{1,0:T(4,128)} custom-call(f32[128,8,128]{2,1,0:T(8,128)} %bitcast.2, f32[3,256]{1,0:T(4,128)} %colour_ref.1, f32[1,256]{1,0:T(1,128)} %bitcast.3, s32[4,64]{1,0:T(4,128)} %order_ref.1), custom_call_target="tpu_custom_call" | custom-call | tf_op jit(solution)/shard_map/pallas_call | solution.py:100

commit v15 on v14

--- a/solution.py
+++ b/solution.py
@@ -106,33 +106,11 @@
     )(tiles, colour_table, opacity_table.reshape(1, -1), depth_order)
 
 
-def arrange_kernel(block, bricks_ref, out_ref):
+def exchange_kernel(bricks_ref, out_ref, send_ref, landed, send_sem, recv_sem, own_sem, arrange_sems):
+    devices, chunk, lanes = landed.shape
     depth, height, width = bricks_ref.shape
-    per_row = width // block
-    parts = block // LANES
-    chunk = depth * parts
-    for s in range(depth):
-        for col in range(width // LANES):
-            h, j = divmod(col, parts)
-            for r in range(0, height, 8):
-                start = (per_row * r + h) * chunk + s * parts + j
-                out_ref[pl.ds(start, 8, stride=per_row * chunk), :] = bricks_ref[s, pl.ds(r, 8), pl.ds(col * LANES, LANES)]
-
-
-def arrange(bricks, devices):
-    depth, height, width = bricks.shape
-    block = height * width // devices
-    vmem = pl.BlockSpec(memory_space=pltpu.VMEM)
-    return pl.pallas_call(
-        functools.partial(arrange_kernel, block),
-        out_shape=jax.ShapeDtypeStruct((height * width * depth // LANES, LANES), bricks.dtype),
-        in_specs=[vmem],
-        out_specs=vmem,
-    )(bricks)
-
-
-def exchange_kernel(send_ref, out_ref, landed, send_sem, recv_sem, own_sem):
-    devices, chunk, lanes = landed.shape
+    per_row = send_ref.shape[1]
+    parts = width // per_row // lanes
     members = lax.axis_size("tile")
     me = lax.axis_index("grp") * members + lax.axis_index("tile")
 
@@ -150,13 +128,26 @@
         return carry
 
     lax.fori_loop(1, devices, greet, 0)
+    arranging = []
+    for s in range(depth):
+        for col in range(width // lanes):
+            h, j = divmod(col, parts)
+            copy = pltpu.make_async_copy(
+                bricks_ref.at[s, :, pl.ds(col * lanes, lanes)],
+                send_ref.at[:, h, s * parts + j, :],
+                arrange_sems.at[len(arranging)],
+            )
+            copy.start()
+            arranging.append(copy)
+    for copy in arranging:
+        copy.wait()
     pl.semaphore_wait(barrier, devices - 1)
 
     def send(k, carry):
         peer_g, peer_t = peer(k)
         dest = peer_g * members + peer_t
         pltpu.make_async_remote_copy(
-            src_ref=send_ref.at[pl.ds(dest * chunk, chunk)],
+            src_ref=send_ref.at[dest // per_row, dest % per_row],
             dst_ref=landed.at[me],
             send_sem=send_sem,
             recv_sem=recv_sem,
@@ -166,7 +157,7 @@
         return carry
 
     lax.fori_loop(1, devices, send, 0)
-    own = pltpu.make_async_copy(send_ref.at[pl.ds(me * chunk, chunk)], landed.at[me], own_sem)
+    own = pltpu.make_async_copy(send_ref.at[me // per_row, me % per_row], landed.at[me], own_sem)
     own.start()
     own.wait()
     everything = pltpu.make_async_remote_copy(
@@ -182,30 +173,34 @@
     out_ref[...] = landed[...]
 
 
-def exchange(flat, devices):
-    chunk = flat.shape[0] // devices
-    shape = (devices, chunk, flat.shape[1])
+def exchange(bricks, devices):
+    depth, height, width = bricks.shape
+    block = height * width // devices
+    per_row = width // block
+    chunk = depth * block // LANES
+    shape = (devices, chunk, LANES)
     return pl.pallas_call(
         exchange_kernel,
-        out_shape=jax.ShapeDtypeStruct(shape, flat.dtype),
+        out_shape=jax.ShapeDtypeStruct(shape, bricks.dtype),
         in_specs=[pl.BlockSpec(memory_space=pltpu.VMEM)],
         out_specs=pl.BlockSpec(memory_space=pltpu.VMEM),
         scratch_shapes=[
-            pltpu.VMEM(shape, flat.dtype),
+            pltpu.VMEM((height, per_row, chunk, LANES), bricks.dtype),
+            pltpu.VMEM(shape, bricks.dtype),
             pltpu.SemaphoreType.DMA,
             pltpu.SemaphoreType.DMA,
             pltpu.SemaphoreType.DMA,
+            pltpu.SemaphoreType.DMA((depth * width // LANES,)),
         ],
         compiler_params=pltpu.CompilerParams(collective_id=0, has_side_effects=True),
-    )(flat)
+    )(bricks)
 
 
 def body(bricks, colour_table, opacity_table, depth_order):
     groups = lax.axis_size("grp")
     members = lax.axis_size("tile")
     devices = groups * members
-    flat = arrange(bricks, devices)
-    arrived = exchange(flat, devices)
+    arrived = exchange(bricks, devices)
     return render(arrived, colour_table, opacity_table, depth_order)
 
 

time: 40.6 us -> 38.3 us (0.943)
  Pallas kernels: 40.4 us -> 38.2 us
    pallas_call x2 -> x1, Pallas kernels: 35.4 us -> 33.2 us  [exchange(): pl.pallas_call(exchange_kernel, out_shape=jax.ShapeDtypeStruct(shape, bri...]
where the time goes in v15:
time: 38.3 us; the launch traced here: 38.2 us
  Pallas kernels  38.2 us (100%)
    pallas_call x1, Pallas kernels, exchange(): pl.pallas_call(exchange_kernel, out_shape=jax.ShapeDtypeStruct(shape, bri...  33.2 us
    pallas_call x1, Pallas kernels, render(): pl.pallas_call(functools.partial(render_kernel, members), out_shape=jax.S...  5.01 us

profile of v15, /device:TPU:1, one launch (start us, length us, event | category | flops | bytes accessed | tf_op | source)
XLA Modules:
  0.0 38.2 jit_solution(12196085176676596036)
XLA Ops:
  0.0 33.2 %shard_map.46 = f32[256,4,128]{2,1,0:T(4,128)} custom-call(f32[2,128,512]{2,1,0:T(8,128)} %bricks_ref.1), custom_call_target="tpu_custom_call" | custom-call | tf_op jit(solution)/shard_map/pallas_call | solution.py:182
  33.2 5.0 %shard_map.47 = f32[4,256]{1,0:T(4,128)} custom-call(f32[128,8,128]{2,1,0:T(8,128)} %bitcast.2, f32[3,256]{1,0:T(4,128)} %colour_ref.1, f32[1,256]{1,0:T(1,128)} %bitcast.3, s32[4,64]{1,0:T(4,128)} %order_ref.1), custom_call_target="tpu_custom_call" | custom-call | tf_op jit(solution)/shard_map/pallas_call | solution.py:100

commit v16 on v15

--- a/solution.py
+++ b/solution.py
@@ -106,7 +106,7 @@
     )(tiles, colour_table, opacity_table.reshape(1, -1), depth_order)
 
 
-def exchange_kernel(bricks_ref, out_ref, send_ref, landed, send_sem, recv_sem, own_sem, arrange_sems):
+def exchange_kernel(bricks_ref, landed, send_ref, send_sem, recv_sem, own_sem, arrange_sems):
     devices, chunk, lanes = landed.shape
     depth, height, width = bricks_ref.shape
     per_row = send_ref.shape[1]
@@ -170,7 +170,6 @@
     )
     everything.wait_send()
     everything.wait_recv()
-    out_ref[...] = landed[...]
 
 
 def exchange(bricks, devices):
@@ -186,7 +185,6 @@
         out_specs=pl.BlockSpec(memory_space=pltpu.VMEM),
         scratch_shapes=[
             pltpu.VMEM((height, per_row, chunk, LANES), bricks.dtype),
-            pltpu.VMEM(shape, bricks.dtype),
             pltpu.SemaphoreType.DMA,
             pltpu.SemaphoreType.DMA,
             pltpu.SemaphoreType.DMA,

time: 38.3 us -> 38.3 us (level)
  no operation moved by 1% of the time
where the time goes in v16:
time: 38.3 us; the launch traced here: 38.1 us
  Pallas kernels  38.1 us (99%)
    pallas_call x1, Pallas kernels, exchange(): pl.pallas_call(exchange_kernel, out_shape=jax.ShapeDtypeStruct(shape, bri...  33.1 us
    pallas_call x1, Pallas kernels, render(): pl.pallas_call(functools.partial(render_kernel, members), out_shape=jax.S...  5.01 us

profile of v16, /device:TPU:1, one launch (start us, length us, event | category | flops | bytes accessed | tf_op | source)
XLA Modules:
  0.0 38.1 jit_solution(4013995373868243160)
XLA Ops:
  0.0 33.1 %shard_map.46 = f32[256,4,128]{2,1,0:T(4,128)} custom-call(f32[2,128,512]{2,1,0:T(8,128)} %bricks_ref.1), custom_call_target="tpu_custom_call" | custom-call | tf_op jit(solution)/shard_map/pallas_call | solution.py:181
  33.1 5.0 %shard_map.47 = f32[4,256]{1,0:T(4,128)} custom-call(f32[128,8,128]{2,1,0:T(8,128)} %bitcast.2, f32[3,256]{1,0:T(4,128)} %colour_ref.1, f32[1,256]{1,0:T(1,128)} %bitcast.3, s32[4,64]{1,0:T(4,128)} %order_ref.1), custom_call_target="tpu_custom_call" | custom-call | tf_op jit(solution)/shard_map/pallas_call | solution.py:100

commit v17 on v15

--- a/solution.py
+++ b/solution.py
@@ -67,7 +67,7 @@
                 parts_ref[c, place] = part[c] if e == 0 else pltpu.roll(part[c], sub - 4, 0)
         return carry
 
-    lax.fori_loop(0, tiles, shade, 0, unroll=32)
+    lax.fori_loop(0, tiles, shade, 0, unroll=64)
 
     def blend(k, pics):
         out = []
@@ -79,7 +79,7 @@
 
     zero = jnp.zeros((sub, lanes), jnp.float32)
     start = tuple(tuple(zero for _ in range(colours + 1)) for _ in range(groups))
-    pics = lax.fori_loop(0, members, blend, start, unroll=8)
+    pics = lax.fori_loop(0, members, blend, start, unroll=16)
     final = pics[0]
     for g in range(1, groups):
         clear = 1.0 - final[colours]

time: 38.3 us -> 38.1 us (level)
  no operation moved by 1% of the time
where the time goes in v17:
time: 38.1 us; the launch traced here: 38 us
  Pallas kernels  38 us (100%)
    pallas_call x1, Pallas kernels, exchange(): pl.pallas_call(exchange_kernel, out_shape=jax.ShapeDtypeStruct(shape, bri...  33.2 us
    pallas_call x1, Pallas kernels, render(): pl.pallas_call(functools.partial(render_kernel, members), out_shape=jax.S...  4.82 us

profile of v17, /device:TPU:1, one launch (start us, length us, event | category | flops | bytes accessed | tf_op | source)
XLA Modules:
  0.0 38.0 jit_solution(11011714841962500929)
XLA Ops:
  0.0 33.2 %shard_map.46 = f32[256,4,128]{2,1,0:T(4,128)} custom-call(f32[2,128,512]{2,1,0:T(8,128)} %bricks_ref.1), custom_call_target="tpu_custom_call" | custom-call | tf_op jit(solution)/shard_map/pallas_call | solution.py:182
  33.2 4.8 %shard_map.47 = f32[4,256]{1,0:T(4,128)} custom-call(f32[128,8,128]{2,1,0:T(8,128)} %bitcast.2, f32[3,256]{1,0:T(4,128)} %colour_ref.1, f32[1,256]{1,0:T(1,128)} %bitcast.3, s32[4,64]{1,0:T(4,128)} %order_ref.1), custom_call_target="tpu_custom_call" | custom-call | tf_op jit(solution)/shard_map/pallas_call | solution.py:100

commit v18 on v17

--- a/solution.py
+++ b/solution.py
@@ -124,7 +124,7 @@
     barrier = pltpu.get_barrier_semaphore()
 
     def greet(k, carry):
-        pl.semaphore_signal(barrier, 1, device_id=peer(k), device_id_type=pl.DeviceIdType.MESH)
+        pl.semaphore_signal(barrier, 1, device_id=peer(devices - k), device_id_type=pl.DeviceIdType.MESH)
         return carry
 
     lax.fori_loop(1, devices, greet, 0)

time: 38.1 us -> 39.2 us (1.029)
  Pallas kernels: 38 us -> 39 us
    pallas_call x1, Pallas kernels: 33.2 us -> 34.2 us  [exchange(): pl.pallas_call(exchange_kernel, out_shape=jax.ShapeDtypeStruct(shape, bri...]
where the time goes in v18:
time: 39.2 us; the launch traced here: 39 us
  Pallas kernels  39 us (99%)
    pallas_call x1, Pallas kernels, exchange(): pl.pallas_call(exchange_kernel, out_shape=jax.ShapeDtypeStruct(shape, bri...  34.2 us
    pallas_call x1, Pallas kernels, render(): pl.pallas_call(functools.partial(render_kernel, members), out_shape=jax.S...  4.82 us

profile of v18, /device:TPU:1, one launch (start us, length us, event | category | flops | bytes accessed | tf_op | source)
XLA Modules:
  0.0 39.0 jit_solution(8515122979388119077)
XLA Ops:
  0.0 34.2 %shard_map.46 = f32[256,4,128]{2,1,0:T(4,128)} custom-call(f32[2,128,512]{2,1,0:T(8,128)} %bricks_ref.1), custom_call_target="tpu_custom_call" | custom-call | tf_op jit(solution)/shard_map/pallas_call | solution.py:182
  34.2 4.8 %shard_map.47 = f32[4,256]{1,0:T(4,128)} custom-call(f32[128,8,128]{2,1,0:T(8,128)} %bitcast.2, f32[3,256]{1,0:T(4,128)} %colour_ref.1, f32[1,256]{1,0:T(1,128)} %bitcast.3, s32[4,64]{1,0:T(4,128)} %order_ref.1), custom_call_target="tpu_custom_call" | custom-call | tf_op jit(solution)/shard_map/pallas_call | solution.py:100

commit v19 on v17

--- a/solution.py
+++ b/solution.py
@@ -67,7 +67,7 @@
                 parts_ref[c, place] = part[c] if e == 0 else pltpu.roll(part[c], sub - 4, 0)
         return carry
 
-    lax.fori_loop(0, tiles, shade, 0, unroll=64)
+    lax.fori_loop(0, tiles, shade, 0, unroll=128)
 
     def blend(k, pics):
         out = []
@@ -79,7 +79,7 @@
 
     zero = jnp.zeros((sub, lanes), jnp.float32)
     start = tuple(tuple(zero for _ in range(colours + 1)) for _ in range(groups))
-    pics = lax.fori_loop(0, members, blend, start, unroll=16)
+    pics = lax.fori_loop(0, members, blend, start, unroll=64)
     final = pics[0]
     for g in range(1, groups):
         clear = 1.0 - final[colours]

time: 38.1 us -> 38 us (level)
  no operation moved by 1% of the time
where the time goes in v19:
time: 38 us; the launch traced here: 37.8 us
  Pallas kernels  37.8 us (99%)
    pallas_call x1, Pallas kernels, exchange(): pl.pallas_call(exchange_kernel, out_shape=jax.ShapeDtypeStruct(shape, bri...  33.2 us
    pallas_call x1, Pallas kernels, render(): pl.pallas_call(functools.partial(render_kernel, members), out_shape=jax.S...  4.67 us

profile of v19, /device:TPU:1, one launch (start us, length us, event | category | flops | bytes accessed | tf_op | source)
XLA Modules:
  0.0 37.8 jit_solution(17932700856570442719)
XLA Ops:
  0.0 33.2 %shard_map.46 = f32[256,4,128]{2,1,0:T(4,128)} custom-call(f32[2,128,512]{2,1,0:T(8,128)} %bricks_ref.1), custom_call_target="tpu_custom_call" | custom-call | tf_op jit(solution)/shard_map/pallas_call | solution.py:182
  33.2 4.7 %shard_map.47 = f32[4,256]{1,0:T(4,128)} custom-call(f32[128,8,128]{2,1,0:T(8,128)} %bitcast.2, f32[3,256]{1,0:T(4,128)} %colour_ref.1, f32[1,256]{1,0:T(1,128)} %bitcast.3, s32[4,64]{1,0:T(4,128)} %order_ref.1), custom_call_target="tpu_custom_call" | custom-call | tf_op jit(solution)/shard_map/pallas_call | solution.py:100
